TPU v7x, 512 devices: a whole 4x4x16 slice. The times are simulated.
512 devices in a mesh: dp: 4 (over z_lo), row: 8 (over y, core), col: 16 (over z_hi, x).
Axes of the slice: x: 4, y: 4, z: 16 (z_hi: 4, z_lo: 4; z = z_hi * 4 + z_lo), core: 2. Of those that a mesh axis runs over, the one named last changes fastest.
Arguments:
- queries: bfloat16 [4, 64, 256, 768], P('dp', 'row', 'col'), may hold values from -5.5 to 5.5
- keys: bfloat16 [4, 64, 256, 768], P('dp', 'row', 'col'), may hold values from -5.5 to 5.5
- values: bfloat16 [4, 64, 256, 768], P('dp', 'row', 'col'), may hold values from -6 to 6
- occupancy: int32 [4, 8, 32], P('dp', 'row', 'col'), may hold values from 0 to 64, as said below
- out_weight: bfloat16 [768, 768], P('dp'), may hold values from -0.21875 to 0.21875
- grad_out: bfloat16 [4, 64, 256, 768], P('dp', 'row', 'col'), may hold values from -6 to 6
Outputs:
- grad_queries: bfloat16 [4, 64, 256, 768], P('dp', 'row', 'col')
- grad_keys: bfloat16 [4, 64, 256, 768], P('dp', 'row', 'col')
- grad_values: bfloat16 [4, 64, 256, 768], P('dp', 'row', 'col')
- grad_weight: float32 [768, 768], P('dp')
Inputs may be any that keep to these rules, and one draw needn't show every extreme that they name: `occupancy`: the occupied tiles of a block are its first that many tiles, row by row over its 8 x 8 tiles. Every slide has a block holding 8 * 8 and a block holding 0.
All inputs are finite; a program needn't handle non-finite values.
Results may differ from a plain program's by a relative error of at most 0.02.
Values may be sent and summed in bfloat16 or wider, within the bound.
A program may use at most 64 MiB of HBM per device.

v0:
```python
import jax
import jax.numpy as jnp
from jax import lax
from jax.sharding import PartitionSpec as P

HEAD_DIM = 64
SIDE = 8
REACH = 3


NEG = -1e30


def passed_along(value, axis, steps):
    count = lax.axis_size(axis)
    leading, last = (max(0, -steps), min(count, count - steps))
    return lax.ppermute(value, axis, [(source, source + steps) for source in range(leading, last)])


def for_sending(value):
    return jax.tree.map(lambda a: a.astype(jnp.bfloat16) if a.dtype == jnp.float32 else a, value)


def extended(cells, sides, width):
    for axis, dim in sides:
        count = lax.axis_size(axis)
        ends = count - 1
        head = lax.slice_in_dim(cells, 0, width, axis=dim)
        tail = lax.slice_in_dim(cells, cells.shape[dim] - width, cells.shape[dim], axis=dim)
        cells = jnp.concatenate(
            [
                lax.ppermute(tail, axis, [(i, (i + 1) % count) for i in range(ends)]),
                cells,
                lax.ppermute(head, axis, [((i + 1) % count, i) for i in range(ends)]),
            ],
            axis=dim,
        )
    return cells


def product(form, left, right):
    return jnp.einsum(form, left, right, preferred_element_type=jnp.float32)


def near_table(block_side, radius):
    window = block_side + 2 * radius
    queries_at = jnp.arange(block_side * block_side)
    keys_at = jnp.arange(window * window)
    row_gap = keys_at[None, :] // window - queries_at[:, None] // block_side - radius
    col_gap = keys_at[None, :] % window - queries_at[:, None] % block_side - radius
    return (jnp.abs(row_gap) <= radius) & (jnp.abs(col_gap) <= radius)


def tile_valid(counts, block_side):
    inside = jnp.arange(block_side * block_side, dtype=jnp.int32).reshape(block_side, block_side)
    flags = inside[None, :, None, :] < counts[:, None, :, None]
    return flags.reshape(counts.shape[0] * block_side, counts.shape[1] * block_side).astype(
        jnp.float32
    )


def blockify(source, block_side):
    height, breadth = (source.shape[0], source.shape[1])
    others = source.shape[2:]
    shaped = source.reshape(
        (height // block_side, block_side, breadth // block_side, block_side) + others
    )
    shaped = jnp.swapaxes(shaped, 1, 2)
    return shaped.reshape(
        (height // block_side, breadth // block_side, block_side * block_side) + others
    )


def unblock(source, block_side):
    block_rows, block_cols = (source.shape[0], source.shape[1])
    others = source.shape[3:]
    shaped = source.reshape((block_rows, block_cols, block_side, block_side) + others)
    shaped = jnp.swapaxes(shaped, 1, 2)
    return shaped.reshape((block_rows * block_side, block_cols * block_side) + others)


def cut_axis(source, dimension, block_side, radius, number):
    padding = [(0, 0)] * source.ndim
    padding[dimension] = (0, block_side - 2 * radius)
    shaped = jnp.pad(source, padding)
    shaped = shaped.reshape(
        source.shape[:dimension] + (number + 1, block_side) + source.shape[dimension + 1 :]
    )
    leading = lax.slice_in_dim(shaped, 0, number, axis=dimension)
    trailing = lax.slice_in_dim(
        lax.slice_in_dim(shaped, 1, number + 1, axis=dimension), 0, 2 * radius, axis=dimension + 1
    )
    return jnp.concatenate([leading, trailing], axis=dimension + 1)


def windows(source, block_side, radius, block_rows, block_cols):
    window = block_side + 2 * radius
    shaped = cut_axis(source, 0, block_side, radius, block_rows)
    shaped = cut_axis(shaped, 2, block_side, radius, block_cols)
    shaped = jnp.swapaxes(shaped, 1, 2)
    return shaped.reshape((block_rows * block_cols, window * window) + source.shape[2:])


def merge_axis(source, dimension, block_side, radius, number):
    leading = lax.slice_in_dim(source, 0, block_side, axis=dimension + 1)
    trailing = lax.slice_in_dim(source, block_side, block_side + 2 * radius, axis=dimension + 1)
    lead_pad = [(0, 0)] * source.ndim
    lead_pad[dimension] = (0, 1)
    trail_pad = [(0, 0)] * source.ndim
    trail_pad[dimension] = (1, 0)
    trail_pad[dimension + 1] = (0, block_side - 2 * radius)
    summed = jnp.pad(leading, lead_pad) + jnp.pad(trailing, trail_pad)
    summed = summed.reshape(
        source.shape[:dimension] + ((number + 1) * block_side,) + source.shape[dimension + 2 :]
    )
    return lax.slice_in_dim(summed, 0, number * block_side + 2 * radius, axis=dimension)


def fold_back(source, block_side, radius, block_rows, block_cols):
    window = block_side + 2 * radius
    shaped = source.reshape((block_rows, block_cols, window, window) + source.shape[2:])
    shaped = jnp.swapaxes(shaped, 1, 2)
    shaped = merge_axis(shaped, 2, block_side, radius, block_cols)
    return merge_axis(shaped, 0, block_side, radius, block_rows)


def attend(query_blocks, key_win, value_win, key_flag, query_flag, nearby, scaling):
    scores = product("nqhd,nkhd->nhqk", query_blocks, key_win) * scaling
    allowed = nearby[None, None] & (key_flag[:, None, None, :] > 0)
    masked = jnp.where(allowed, scores, NEG)
    highest = jnp.max(masked, axis=-1, keepdims=True)
    raised = jnp.exp(masked - highest)
    inverse = 1.0 / jnp.sum(raised, axis=-1, keepdims=True)
    weights = raised * inverse
    rounded = weights.astype(jnp.bfloat16)
    mixed = product("nhqk,nkhd->nqhd", rounded, value_win)
    attended = (mixed * query_flag[:, :, None, None]).astype(jnp.bfloat16)
    return (attended, weights, rounded, highest, inverse)


def query_side(weights, grad_blocks, key_win, value_win, scaling):
    prob_grad = product("nqhd,nkhd->nhqk", grad_blocks, value_win)
    correction = jnp.sum(weights * prob_grad, axis=-1, keepdims=True)
    score_grad = (weights * (prob_grad - correction) * scaling).astype(jnp.bfloat16)
    query_grad = product("nhqk,nkhd->nqhd", score_grad, key_win)
    return (query_grad, score_grad, correction)


def return_rims(key_full, value_full):
    middle = (key_full[REACH:-REACH], value_full[REACH:-REACH])
    for offset in (1, -1):
        if offset == 1:
            border = (key_full[-REACH:], value_full[-REACH:])
        else:
            border = (key_full[:REACH], value_full[:REACH])
        arrived = (
            passed_along(border[0].astype(jnp.bfloat16), "row", offset).astype(jnp.float32),
            passed_along(border[1].astype(jnp.bfloat16), "row", offset).astype(jnp.float32),
        )
        if offset == 1:
            middle = tuple(
                (portion.at[:REACH].add(incoming) for portion, incoming in zip(middle, arrived))
            )
        else:
            middle = tuple(
                (portion.at[-REACH:].add(incoming) for portion, incoming in zip(middle, arrived))
            )
    centre = tuple((portion[:, REACH:-REACH] for portion in middle))
    for offset in (1, -1):
        if offset == 1:
            border = tuple((portion[:, -REACH:] for portion in middle))
        else:
            border = tuple((portion[:, :REACH] for portion in middle))
        arrived = jax.tree.map(
            lambda part, own: part.astype(own.dtype),
            passed_along(for_sending(border), "col", offset),
            border,
        )
        if offset == 1:
            centre = tuple(
                (portion.at[:, :REACH].add(incoming) for portion, incoming in zip(centre, arrived))
            )
        else:
            centre = tuple(
                (portion.at[:, -REACH:].add(incoming) for portion, incoming in zip(centre, arrived))
            )
    return centre


def on_device(queries, keys, values, occupancy, out_weight, grad_out):
    query_tiles = queries[0]
    key_tiles = keys[0]
    value_tiles = values[0]
    grad_tiles = grad_out[0]
    counts = occupancy[0]
    height, breadth, channels = query_tiles.shape
    out_width = grad_tiles.shape[2]
    head_count = channels // HEAD_DIM
    block_rows = height // SIDE
    block_cols = breadth // SIDE
    block_count = block_rows * block_cols
    block_area = SIDE * SIDE
    window = SIDE + 2 * REACH
    window_area = window * window
    tile_count = height * breadth
    nearby = near_table(SIDE, REACH)
    scaling = HEAD_DIM ** (-0.5)
    occupied = tile_valid(counts, SIDE)
    key_ext, value_ext, flag_ext = (
        extended(key_tiles, (("row", 0), ("col", 1)), REACH),
        extended(value_tiles, (("row", 0), ("col", 1)), REACH),
        extended(occupied.astype(jnp.bfloat16), (("row", 0), ("col", 1)), REACH),
    )
    key_win = windows(key_ext, SIDE, REACH, block_rows, block_cols).reshape(
        block_count, window_area, head_count, HEAD_DIM
    )
    value_win = windows(value_ext, SIDE, REACH, block_rows, block_cols).reshape(
        block_count, window_area, head_count, HEAD_DIM
    )
    flag_win = windows(flag_ext, SIDE, REACH, block_rows, block_cols)
    query_blocks = blockify(query_tiles, SIDE).reshape(
        block_count, block_area, head_count, HEAD_DIM
    )
    query_flag = blockify(occupied, SIDE).reshape(block_count, block_area)
    attended, weights, rounded, highest, inverse = attend(
        query_blocks, key_win, value_win, flag_win, query_flag, nearby, scaling
    )
    flat_grads = grad_tiles.reshape(tile_count, out_width)
    out_back = lax.dot_general(
        flat_grads,
        lax.all_gather(out_weight, "dp", axis=0, tiled=True),
        (((1,), (1,)), ((), ())),
        preferred_element_type=jnp.float32,
    )
    gated_grad = out_back.astype(jnp.bfloat16).reshape(height, breadth, channels) * occupied[
        :, :, None
    ].astype(jnp.bfloat16)
    grad_blocks = blockify(gated_grad, SIDE).reshape(block_count, block_area, head_count, HEAD_DIM)
    out_blocks = blockify(grad_tiles, SIDE).reshape(tile_count, out_width)
    weight_term = lax.dot_general(
        attended.reshape(tile_count, channels),
        out_blocks,
        (((0,), (0,)), ((), ())),
        preferred_element_type=jnp.float32,
    )
    summed = lax.psum(weight_term, ("row", "col"))
    slide_part = lax.psum_scatter(
        summed.astype(jnp.bfloat16), "dp", scatter_dimension=0, tiled=True
    ).astype(jnp.float32)
    all_tiles = tile_count * lax.axis_size("dp") * lax.axis_size("row") * lax.axis_size("col")
    grad_weight = slide_part * all_tiles ** (-0.5)
    query_grad, score_grad, correction = query_side(
        weights, grad_blocks, key_win, value_win, scaling
    )
    key_part = product("nhqk,nqhd->nkhd", score_grad, query_blocks).reshape(
        block_count, window_area, channels
    )
    value_part = product("nhqk,nqhd->nkhd", rounded, grad_blocks).reshape(
        block_count, window_area, channels
    )
    key_full = fold_back(key_part, SIDE, REACH, block_rows, block_cols)
    value_full = fold_back(value_part, SIDE, REACH, block_rows, block_cols)
    key_sum, value_sum = return_rims(key_full, value_full)
    grad_query = unblock(query_grad.reshape(block_rows, block_cols, block_area, channels), SIDE)
    return (
        grad_query.astype(jnp.bfloat16)[None],
        key_sum.astype(jnp.bfloat16)[None],
        value_sum.astype(jnp.bfloat16)[None],
        grad_weight,
    )


def solution(mesh):
    return jax.shard_map(
        on_device,
        mesh=mesh,
        in_specs=(
            P("dp", "row", "col", None),
            P("dp", "row", "col", None),
            P("dp", "row", "col", None),
            P("dp", "row", "col"),
            P("dp", None),
            P("dp", "row", "col", None),
        ),
        out_specs=(
            P("dp", "row", "col", None),
            P("dp", "row", "col", None),
            P("dp", "row", "col", None),
            P("dp", None),
        ),
        check_vma=False,
    )
```

profile of v0, /device:TPU:46, one launch (start us, length us, event | category | flops | bytes accessed | tf_op | source)
XLA Modules:
  0.0 1017.9 jit_solution(9643661524782293680)
XLA Ops:
  10.2 2.4 collective-permute-start
  13.7 3.2 collective-permute-start.9
  19.7 2.4 collective-permute-start.4
  25.9 2.7 collective-permute-start.7
  28.7 9.1 collective-permute-start.6
  37.8 2.5 collective-permute-start.8
  42.9 9.9 collective-permute-start.2
  54.9 9.9 collective-permute-start.10
  66.4 9.1 collective-permute-done.11
  80.1 2.4 fusion.67
  87.6 4.9 fusion.24
  95.3 755.2 %all-reduce.15 = bf16[768,768]{1,0:T(8,128)(2,1)} all-reduce(f32[768,768]{1,0:T(8,128)S(1)} %fusion.69), channel_id=1, replica_groups=mesh['dp'=4,'row'=8,'col'=16] {'row','col'}, use_global_device_ids=true, to_apply=%region_3.4 | all-reduce | flops 589824 | bytes 3538944 | tf_op jit(solution)/shard_map/psum | solution.py:246
  854.9 11.5 %fusion.25 = bf16[2,64,12,64]{1,3,2,0:T(8,128)(2,1)} fusion(bf16[2,196,12,64]{1,3,2,0:T(8,128)(2,1)S(1)} %copy.80, f32[2,12,64,196]{3,2,1,0:T(8,128)} %fusion.68, f32[2,12,64,196]{3,2,1,0:T(8,128)} %get-tuple-element.127, f32[2,12,64]{2,1,0:T(8,128)S(1)} %broadcast_divide_fusion), kind=kOutput, calls=%fused_computation.21 | convolution fusion | flops 40742596 | bytes 3213312 | tf_op jit(solution)/shard_map/nhqk,nkhd->nqhd/dot_general | solution.py:42
  866.4 11.9 %fusion.12 = f32[2,196,12,64]{1,3,2,0:T(8,128)} fusion(bf16[2,64,12,64]{1,3,2,0:T(8,128)(2,1)S(1)} %copy-done.10, f32[2,12,64,196]{3,2,1,0:T(8,128)} %fusion.68, f32[2,12,64,196]{3,2,1,0:T(8,128)} %get-tuple-element.127, f32[2,12,64]{2,1,0:T(8,128)S(1)} %broadcast_divide_fusion), kind=kOutput, calls=%fused_computation.9 | convolution fusion | flops 40644292 | bytes 3815424 | tf_op jit(solution)/shard_map/nhqk,nqhd->nkhd/dot_general | solution.py:42
  878.3 3.5 copy.84
  888.5 5.8 convolution_bitcast_fusion
  894.3 3.5 copy.87
  897.8 2.2 reshape_reshape.27
  907.7 11.2 %collective-permute-start.13 = (bf16[3,22,768]{2,1,0:T(8,128)(2,1)S(1)}, bf16[3,22,768]{2,1,0:T(8,128)(2,1)S(1)}, u32[]{:S(2)}, u32[]{:S(2)}) collective-permute-start(bf16[3,22,768]{2,1,0:T(8,128)(2,1)S(1)} %get-tuple-element.102), channel_id=1, source_target_pairs={{16,0},{32,16},{48,32},{64,48},{80,64},{96,80},{112,96},{17,1},{33... | collective-permute-start | bytes 304136 | tf_op jit(solution)/shard_map/ppermute | solution.py:17
  920.9 51.0 %collective-permute-start.17 = (bf16[3,22,768]{2,1,0:T(8,128)(2,1)S(1)}, bf16[3,22,768]{2,1,0:T(8,128)(2,1)S(1)}, u32[]{:S(2)}, u32[]{:S(2)}) collective-permute-start(bf16[3,22,768]{2,1,0:T(8,128)(2,1)S(1)} %get-tuple-element.100), channel_id=1, source_target_pairs={{16,0},{32,16},{48,32},{64,48},{80,64},{96,80},{112,96},{17,1},{33... | collective-permute-start | bytes 304136 | tf_op jit(solution)/shard_map/ppermute | solution.py:17
  974.3 9.3 collective-permute-start.14
  983.6 3.1 collective-permute-start.15
  986.8 8.7 collective-permute-start.18
  998.7 8.8 collective-permute-done.19
  (182 shorter events, 58.5 us)
Async XLA Ops:
  7.2 843.3 %all-gather.2.cloned.1.call-start = ((), (), s32[]{:S(2)}) async-start(), calls=%async_computation.1 | async-start | bytes 1474560 | tf_op jit(solution)/shard_map/all_gather | solution.py:231
  8.3 32.6 %collective-permute-start.1 = (bf16[3,16,768]{2,1,0:T(8,128)(2,1)S(1)}, bf16[3,16,768]{2,1,0:T(8,128)(2,1)S(1)}, u32[]{:S(2)}, u32[]{:S(2)}) collective-permute-start(bf16[3,16,768]{2,1,0:T(8,128)(2,1)S(1)} %get-tuple-element.119), channel_id=1, source_target_pairs={{16,0},{32,16},{48,32},{64,48},{80,64},{96,80},{112,96},{17,1},{33... | collective-permute-start | bytes 221192 | tf_op jit(solution)/shard_map/ppermute | solution.py:34
  10.2 30.7 %collective-permute-start = (bf16[3,16,768]{2,1,0:T(8,128)(2,1)S(1)}, bf16[3,16,768]{2,1,0:T(8,128)(2,1)S(1)}, u32[]{:S(2)}, u32[]{:S(2)}) collective-permute-start(bf16[3,16,768]{2,1,0:T(8,128)(2,1)S(1)} %get-tuple-element.118), channel_id=1, source_target_pairs={{0,16},{16,32},{32,48},{48,64},{64,80},{80,96},{96,112},{1,17},{17... | collective-permute-start | bytes 221192 | tf_op jit(solution)/shard_map/ppermute | solution.py:32
  12.7 996.6 %reduce-scatter.2.cloned.1.call-start = ((), (), s32[]{:S(2)}) async-start(), calls=%async_computation.2 | async-start | bytes 1474560 | tf_op jit(solution)/shard_map/reduce_scatter | solution.py:247
  13.7 39.2 %collective-permute-start.9 = (bf16[3,16,768]{2,1,0:T(8,128)(2,1)S(1)}, bf16[3,16,768]{2,1,0:T(8,128)(2,1)S(1)}, u32[]{:S(2)}, u32[]{:S(2)}) collective-permute-start(bf16[3,16,768]{2,1,0:T(8,128)(2,1)S(1)} %get-tuple-element.117), channel_id=1, source_target_pairs={{16,0},{32,16},{48,32},{64,48},{80,64},{96,80},{112,96},{17,1},{33... | collective-permute-start | bytes 221192 | tf_op jit(solution)/shard_map/ppermute | solution.py:34
  17.8 8.1 collective-permute-start.5
  19.7 6.2 collective-permute-start.4
  24.9 57.6 %copy-start.9 = (bf16[2,64,12,64]{1,3,2,0:T(8,128)(2,1)}, bf16[2,64,12,64]{1,3,2,0:T(8,128)(2,1)S(1)}, u32[]{:S(2)}) copy-start(bf16[2,64,12,64]{1,3,2,0:T(8,128)(2,1)S(1)} %copy.83) | copy-start | bytes 589828
  25.9 11.9 %collective-permute-start.7 = (bf16[14,3]{1,0:T(8,128)(2,1)S(1)}, bf16[14,3]{1,0:T(8,128)(2,1)S(1)}, u32[]{:S(2)}, u32[]{:S(2)}) collective-permute-start(bf16[14,3]{1,0:T(8,128)(2,1)S(1)} %get-tuple-element.123), channel_id=1, source_target_pairs={{1,0},{2,1},{3,2},{4,3},{5,4},{6,5},{7,6},{8,7},{9,8},{10,9},{11,1... | collective-permute-start | bytes 260 | tf_op jit(solution)/shard_map/ppermute | solution.py:34
  28.7 11.7 %collective-permute-start.6 = (bf16[14,3]{1,0:T(8,128)(2,1)S(1)}, bf16[14,3]{1,0:T(8,128)(2,1)S(1)}, u32[]{:S(2)}, u32[]{:S(2)}) collective-permute-start(bf16[14,3]{1,0:T(8,128)(2,1)S(1)} %get-tuple-element.122), channel_id=1, source_target_pairs={{0,1},{1,2},{2,3},{3,4},{4,5},{5,6},{6,7},{7,8},{8,9},{9,10},{10,1... | collective-permute-start | bytes 260 | tf_op jit(solution)/shard_map/ppermute | solution.py:32
  37.8 15.1 %collective-permute-start.8 = (bf16[3,16,768]{2,1,0:T(8,128)(2,1)S(1)}, bf16[3,16,768]{2,1,0:T(8,128)(2,1)S(1)}, u32[]{:S(2)}, u32[]{:S(2)}) collective-permute-start(bf16[3,16,768]{2,1,0:T(8,128)(2,1)S(1)} %get-tuple-element.116), channel_id=1, source_target_pairs={{0,16},{16,32},{32,48},{48,64},{64,80},{80,96},{96,112},{1,17},{17... | collective-permute-start | bytes 221192 | tf_op jit(solution)/shard_map/ppermute | solution.py:32
  41.0 25.0 %collective-permute-start.3 = (bf16[14,3,768]{2,1,0:T(4,128)(2,1)S(1)}, bf16[14,3,768]{2,1,0:T(4,128)(2,1)S(1)}, u32[]{:S(2)}, u32[]{:S(2)}) collective-permute-start(bf16[14,3,768]{2,1,0:T(4,128)(2,1)S(1)} %get-tuple-element.111), channel_id=1, source_target_pairs={{1,0},{2,1},{3,2},{4,3},{5,4},{6,5},{7,6},{8,7},{9,8},{10,9},{11,1... | collective-permute-start | bytes 193544 | tf_op jit(solution)/shard_map/ppermute | solution.py:34
  42.9 23.1 %collective-permute-start.2 = (bf16[14,3,768]{2,1,0:T(4,128)(2,1)S(1)}, bf16[14,3,768]{2,1,0:T(4,128)(2,1)S(1)}, u32[]{:S(2)}, u32[]{:S(2)}) collective-permute-start(bf16[14,3,768]{2,1,0:T(4,128)(2,1)S(1)} %get-tuple-element.110), channel_id=1, source_target_pairs={{0,1},{1,2},{2,3},{3,4},{4,5},{5,6},{6,7},{7,8},{8,9},{9,10},{10,1... | collective-permute-start | bytes 193544 | tf_op jit(solution)/shard_map/ppermute | solution.py:32
  53.0 22.5 %collective-permute-start.11 = (bf16[14,3,768]{2,1,0:T(4,128)(2,1)S(1)}, bf16[14,3,768]{2,1,0:T(4,128)(2,1)S(1)}, u32[]{:S(2)}, u32[]{:S(2)}) collective-permute-start(bf16[14,3,768]{2,1,0:T(4,128)(2,1)S(1)} %get-tuple-element.109), channel_id=1, source_target_pairs={{1,0},{2,1},{3,2},{4,3},{5,4},{6,5},{7,6},{8,7},{9,8},{10,9},{11,1... | collective-permute-start | bytes 193544 | tf_op jit(solution)/shard_map/ppermute | solution.py:34
  54.9 20.6 %collective-permute-start.10 = (bf16[14,3,768]{2,1,0:T(4,128)(2,1)S(1)}, bf16[14,3,768]{2,1,0:T(4,128)(2,1)S(1)}, u32[]{:S(2)}, u32[]{:S(2)}) collective-permute-start(bf16[14,3,768]{2,1,0:T(4,128)(2,1)S(1)} %get-tuple-element.108), channel_id=1, source_target_pairs={{0,1},{1,2},{2,3},{3,4},{4,5},{5,6},{6,7},{7,8},{8,9},{9,10},{10,1... | collective-permute-start | bytes 193544 | tf_op jit(solution)/shard_map/ppermute | solution.py:32
  95.2 755.3 %copy-start.15 = (bf16[1,8,16,768]{3,2,1,0:T(8,128)(2,1)S(1)}, bf16[1,8,16,768]{3,2,1,0:T(8,128)(2,1)}, u32[]{:S(2)}) copy-start(bf16[1,8,16,768]{3,2,1,0:T(8,128)(2,1)} %param.27) | copy-start | bytes 589828
  905.5 66.3 %collective-permute-start.12 = (bf16[3,22,768]{2,1,0:T(8,128)(2,1)S(1)}, bf16[3,22,768]{2,1,0:T(8,128)(2,1)S(1)}, u32[]{:S(2)}, u32[]{:S(2)}) collective-permute-start(bf16[3,22,768]{2,1,0:T(8,128)(2,1)S(1)} %get-tuple-element.103), channel_id=1, source_target_pairs={{0,16},{16,32},{32,48},{48,64},{64,80},{80,96},{96,112},{1,17},{17... | collective-permute-start | bytes 304136 | tf_op jit(solution)/shard_map/ppermute | solution.py:17
  907.7 64.2 %collective-permute-start.13 = (bf16[3,22,768]{2,1,0:T(8,128)(2,1)S(1)}, bf16[3,22,768]{2,1,0:T(8,128)(2,1)S(1)}, u32[]{:S(2)}, u32[]{:S(2)}) collective-permute-start(bf16[3,22,768]{2,1,0:T(8,128)(2,1)S(1)} %get-tuple-element.102), channel_id=1, source_target_pairs={{16,0},{32,16},{48,32},{64,48},{80,64},{96,80},{112,96},{17,1},{33... | collective-permute-start | bytes 304136 | tf_op jit(solution)/shard_map/ppermute | solution.py:17
  918.9 53.4 %collective-permute-start.16 = (bf16[3,22,768]{2,1,0:T(8,128)(2,1)S(1)}, bf16[3,22,768]{2,1,0:T(8,128)(2,1)S(1)}, u32[]{:S(2)}, u32[]{:S(2)}) collective-permute-start(bf16[3,22,768]{2,1,0:T(8,128)(2,1)S(1)} %get-tuple-element.101), channel_id=1, source_target_pairs={{0,16},{16,32},{32,48},{48,64},{64,80},{80,96},{96,112},{1,17},{17... | collective-permute-start | bytes 304136 | tf_op jit(solution)/shard_map/ppermute | solution.py:17
  920.9 53.3 %collective-permute-start.17 = (bf16[3,22,768]{2,1,0:T(8,128)(2,1)S(1)}, bf16[3,22,768]{2,1,0:T(8,128)(2,1)S(1)}, u32[]{:S(2)}, u32[]{:S(2)}) collective-permute-start(bf16[3,22,768]{2,1,0:T(8,128)(2,1)S(1)} %get-tuple-element.100), channel_id=1, source_target_pairs={{16,0},{32,16},{48,32},{64,48},{80,64},{96,80},{112,96},{17,1},{33... | collective-permute-start | bytes 304136 | tf_op jit(solution)/shard_map/ppermute | solution.py:17
  974.3 23.2 %collective-permute-start.14 = (bf16[8,3,768]{2,1,0:T(4,128)(2,1)S(1)}, bf16[8,3,768]{2,1,0:T(4,128)(2,1)S(1)}, u32[]{:S(2)}, u32[]{:S(2)}) collective-permute-start(bf16[8,3,768]{2,1,0:T(4,128)(2,1)S(1)} %get-tuple-element.115), channel_id=1, source_target_pairs={{0,1},{1,2},{2,3},{3,4},{4,5},{5,6},{6,7},{7,8},{8,9},{9,10},{10,1... | collective-permute-start | bytes 110600 | tf_op jit(solution)/shard_map/ppermute | solution.py:17
  983.6 14.3 %collective-permute-start.15 = (bf16[8,3,768]{2,1,0:T(4,128)(2,1)S(1)}, bf16[8,3,768]{2,1,0:T(4,128)(2,1)S(1)}, u32[]{:S(2)}, u32[]{:S(2)}) collective-permute-start(bf16[8,3,768]{2,1,0:T(4,128)(2,1)S(1)} %get-tuple-element.114), channel_id=1, source_target_pairs={{1,0},{2,1},{3,2},{4,3},{5,4},{6,5},{7,6},{8,7},{9,8},{10,9},{11,1... | collective-permute-start | bytes 110600 | tf_op jit(solution)/shard_map/ppermute | solution.py:17
  986.8 10.7 %collective-permute-start.18 = (bf16[8,3,768]{2,1,0:T(4,128)(2,1)S(1)}, bf16[8,3,768]{2,1,0:T(4,128)(2,1)S(1)}, u32[]{:S(2)}, u32[]{:S(2)}) collective-permute-start(bf16[8,3,768]{2,1,0:T(4,128)(2,1)S(1)} %get-tuple-element.113), channel_id=1, source_target_pairs={{0,1},{1,2},{2,3},{3,4},{4,5},{5,6},{6,7},{7,8},{8,9},{9,10},{10,1... | collective-permute-start | bytes 110600 | tf_op jit(solution)/shard_map/ppermute | solution.py:17
  995.5 12.0 %collective-permute-start.19 = (bf16[8,3,768]{2,1,0:T(4,128)(2,1)S(1)}, bf16[8,3,768]{2,1,0:T(4,128)(2,1)S(1)}, u32[]{:S(2)}, u32[]{:S(2)}) collective-permute-start(bf16[8,3,768]{2,1,0:T(4,128)(2,1)S(1)} %get-tuple-element.112), channel_id=1, source_target_pairs={{1,0},{2,1},{3,2},{4,3},{5,4},{6,5},{7,6},{8,7},{9,8},{10,9},{11,1... | collective-permute-start | bytes 110600 | tf_op jit(solution)/shard_map/ppermute | solution.py:17
  (19 other events, 151.1 us)
Sparse Core Ops, SparseCore 0:
  12.8 43.8 all-gather.1
  850.6 100.3 reduce-scatter.1
where the time goes:
time: 1020 us
  blocking collectives  755 us (74%)
  starting transfers between devices  139 us (14%)
  matrix products  43 us (4%)
  local copies, waits for them, and re-layouts  35 us (3%)
  waiting for transfers between devices  21.3 us (2%)
  between operations  15.1 us (1%)
    psum x1, blocking collectives, on_device(): summed = lax.psum(weight_term, ('row', 'col'))  755 us
    ppermute x8, starting transfers between devices, passed_along(): lax.ppermute(value, axis, [(source, source + steps) for source in range(l...  89 us
    dot_general x6, matrix products, product(): return jnp.einsum(form, left, right, preferred_element_type=jnp.float32)  37.2 us
    ppermute x6, starting transfers between devices, extended(): lax.ppermute(tail, axis, [(i, (i + 1) % count) for i in range(ends)])  36.4 us
  transfers between devices with their start and end apart: 22, of which 5 were waited for; matrix products, arithmetic and copies ran while one was open for 8% of the time, Pallas kernels for 0%

commit v1 on v0

v1 whole, which is shorter than its diff:
```python
import functools

import jax
import jax.numpy as jnp
import numpy as np
from jax import lax
from jax.experimental import pallas as pl
from jax.experimental.pallas import tpu as pltpu
from jax.sharding import PartitionSpec as P

MESH = pl.DeviceIdType.MESH
CH = 768
SIDE = 8
REACH = 3
HIGH = 8
WIDE = 16
TILES = HIGH * WIDE
PAIR = 128
PAIRS = CH // PAIR
HEAD_SCALE = 64 ** (-0.5)
NEG = -1e30
UP, DOWN, SIDES, KEYS = 128, 176, 224, 320
BF = jnp.bfloat16
F32 = jnp.float32


def key_places():
    places = [(i // WIDE, i % WIDE) for i in range(TILES)]
    places += [(i // WIDE - REACH, i % WIDE) for i in range(48)]
    places += [(i // WIDE + HIGH, i % WIDE) for i in range(48)]
    for first in (-REACH, WIDE):
        places += [(j // 3 - REACH, first + j % 3) if j < 42 else None for j in range(48)]
    return places


@functools.lru_cache(None)
def tables():
    places = key_places()
    limit = np.full((KEYS, TILES), 1000.0, np.float32)
    block = np.zeros((KEYS, 96), np.float32)
    for u, place in enumerate(places):
        if place is None:
            continue
        row, column = place
        block[u, 8 * (4 * (row // SIDE + 1) + column // SIDE + 1)] = 1
        for t in range(TILES):
            if abs(t // WIDE - row) <= REACH and abs(t % WIDE - column) <= REACH:
                limit[u, t] = (row % SIDE) * SIDE + column % SIDE
    pack = np.zeros((96, 2 * TILES), np.float32)
    for kind in range(2):
        for side in range(2):
            for r in range(HIGH):
                for c in range(3):
                    pack[48 * side + 24 * kind + 3 * r + c, TILES * kind + WIDE * r + 13 * side + c] = 1

    def strip(side, kind, r, c):
        return 48 * side + 24 * kind + 3 * r + c

    def corner(kind, side, r, c):
        return 18 * kind + 9 * side + 3 * r + c

    corners = np.zeros((96, 96), np.float32)
    sides = np.zeros((192, 192), np.float32)
    back_corners = np.zeros((96, 192), np.float32)
    back_strips = np.zeros((96, 288), np.float32)
    for kind in range(2):
        for side in range(2):
            for c in range(3):
                for r in range(3):
                    at = corner(kind, side, r, c)
                    corners[at, strip(side, kind, r, c)] = 1
                    corners[48 + at, strip(side, kind, r + 5, c)] = 1
                    sides[96 * kind + 48 * side + 3 * r + c, 96 + at] = 1
                    sides[96 * kind + 48 * side + 3 * (r + 11) + c, 144 + at] = 1
                    back_corners[at, 96 * kind + 48 * side + 3 * r + c] = 1
                    back_corners[48 + at, 96 * kind + 48 * side + 3 * (r + 11) + c] = 1
                    back_strips[strip(side, kind, r, c), 192 + at] = 1
                    back_strips[strip(side, kind, r + 5, c), 192 + 48 + at] = 1
                for r in range(HIGH):
                    sides[96 * kind + 48 * side + 3 * (r + 3) + c, strip(side, kind, r, c)] = 1
                    back_strips[strip(side, kind, r, c), 96 * kind + 48 * side + 3 * (r + 3) + c] = 1
    unpack = np.concatenate([pack[:, :TILES].T, pack[:, TILES:].T], axis=0)
    return tuple(
        np.asarray(t, dtype=BF)
        for t in (limit, block, pack, corners, sides, back_corners, back_strips, unpack)
    )


def dot(a, b, dims=((1,), (0,))):
    return lax.dot_general(a, b, (dims, ((), ())), preferred_element_type=F32)


def body(
    sizes,
    q_ref, k_ref, v_ref, go_ref, w_ref, occ_ref,
    limit_ref, block_ref, pack_ref, corners_ref, sides_ref, bcorn_ref, bstrip_ref, unpack_ref,
    dq_ref, dk_ref, dv_ref, gw_ref,
    kall, vall, strips, held, corn, cnt, wfull, bias, prob, attn_t, gated,
    dk_own, dv_own, row_out, row_in, dcol, bcorn, bcorn_in, bstrip, bstrip_in,
    gw_own, core_out, core_in, y_sum, y_out, y_in, x_sum, x_out, x_in, z_out, z_in, h_all, g_all,
    ssem, rsem,
):
    DP, ROWS, COLS, X = sizes
    Y, ZH = ROWS // 2, COLS // X
    Z = DP * ZH
    part = CH // DP
    half = part // 2
    dp, row, col = lax.axis_index("dp"), lax.axis_index("row"), lax.axis_index("col")
    core, y = row % 2, row // 2
    x, zh = col % X, col // X
    z = zh * DP + dp
    has_up, has_down = row > 0, row < ROWS - 1
    has_left, has_right = col > 0, col < COLS - 1
    up, down = (dp, row - 1, col), (dp, row + 1, col)
    left, right = (dp, row, col - 1), (dp, row, col + 1)
    partner = (dp, row + 1 - 2 * core, col)

    def along_z(step):
        there = (z + step + Z) % Z
        return (there % DP, row, (there // DP) * X + x)

    def along_y(step):
        return (dp, ((y + step) % Y) * 2 + core, col)

    def along_x(step):
        return (dp, row, zh * X + (x + step) % X)

    def along_lo(step):
        return ((dp + step) % DP, row, col)

    def along_hi(step):
        return (dp, row, ((zh + step) % ZH) * X + x)

    if DP == 4:
        plan = [(1, 0, half), (-1, 0, half), (2, 0, half // 2), (-2, half // 2, half // 2)]
    else:
        plan = [(1, 0, half // 2), (-1, half // 2, half // 2)]

    kall[pl.ds(UP, 96), :] = jnp.zeros((96, CH), BF)
    vall[pl.ds(UP, 96), :] = jnp.zeros((96, CH), BF)
    held[...] = jnp.zeros(held.shape, BF)
    row_in[...] = jnp.zeros(row_in.shape, BF)
    bcorn_in[...] = jnp.zeros(bcorn_in.shape, BF)
    bstrip_in[...] = jnp.zeros(bstrip_in.shape, BF)
    cnt[...] = jnp.zeros(cnt.shape, F32)

    barrier = pltpu.get_barrier_semaphore()

    def greet(device):
        pl.semaphore_signal(barrier, inc=1, device_id=device, device_id_type=MESH)

    for there, device in ((has_up, up), (has_down, down), (has_left, left), (has_right, right)):
        pl.when(there)(functools.partial(greet, device))
    fixed = [partner] + [along_z(step) for step, _, _ in plan]
    fixed += [along_y(s) for s in range(1, Y)] + [along_x(s) for s in range(1, X)]
    fixed += [along_lo(s) for s in range(1, DP)] + [along_hi(s) for s in range(1, ZH)]
    for device in fixed:
        greet(device)

    count0, count1 = occ_ref[0, 0].astype(F32), occ_ref[0, 1].astype(F32)
    cnt[1, 1] = jnp.full((8, 128), count0, F32)
    cnt[1, 2] = jnp.full((8, 128), count1, F32)
    packed = dot(pack_ref[:, :TILES], k_ref[...]) + dot(pack_ref[:, TILES:], v_ref[...])
    strips[...] = packed.astype(BF)

    around = sum(t.astype(jnp.int32) for t in (has_up, has_down, has_left, has_right))
    pl.semaphore_wait(barrier, around + len(fixed))

    used = [0]

    class Copy:
        def __init__(self, src, dst, device, sends=None, gets=None):
            index = used[0]
            used[0] += 1
            self.sends, self.gets = sends, gets
            self.copy = pltpu.make_async_remote_copy(
                src_ref=src, dst_ref=dst, send_sem=ssem.at[index], recv_sem=rsem.at[index],
                device_id=device, device_id_type=MESH,
            )

        def start(self):
            if self.sends is None:
                self.copy.start()
            else:
                pl.when(self.sends)(lambda: self.copy.start())
            return self

        def arrived(self):
            if self.gets is None:
                self.copy.wait_recv()
            else:
                pl.when(self.gets)(lambda: self.copy.wait_recv())

        def sent(self):
            if self.sends is None:
                self.copy.wait_send()
            else:
                pl.when(self.sends)(lambda: self.copy.wait_send())

    started = []

    def send(*args, **kwargs):
        made = Copy(*args, **kwargs).start()
        started.append(made)
        return made

    to_left = dict(sends=has_left, gets=has_right)
    to_right = dict(sends=has_right, gets=has_left)
    to_up = dict(sends=has_up, gets=has_down)
    to_down = dict(sends=has_down, gets=has_up)
    first = [
        send(cnt.at[1, 1], cnt.at[1, 3], left, **to_left),
        send(cnt.at[1, 2], cnt.at[1, 0], right, **to_right),
        send(strips.at[pl.ds(0, 48)], held.at[pl.ds(48, 48)], left, **to_left),
        send(strips.at[pl.ds(48, 48)], held.at[pl.ds(0, 48)], right, **to_right),
    ]
    rows = [
        send(k_ref.at[pl.ds(0, 48)], kall.at[pl.ds(DOWN, 48)], up, **to_up),
        send(k_ref.at[pl.ds(80, 48)], kall.at[pl.ds(UP, 48)], down, **to_down),
        send(v_ref.at[pl.ds(0, 48)], vall.at[pl.ds(DOWN, 48)], up, **to_up),
        send(v_ref.at[pl.ds(80, 48)], vall.at[pl.ds(UP, 48)], down, **to_down),
    ]
    kall[pl.ds(0, TILES), :] = k_ref[...]
    vall[pl.ds(0, TILES), :] = v_ref[...]
    base = pl.multiple_of(dp * part, 16)
    wfull[pl.ds(base, part), :] = w_ref[...]

    for copy in first:
        copy.arrived()
    corn[...] = dot(corners_ref[...], held[pl.ds(0, 96), :]).astype(BF)
    second = [
        send(corn.at[pl.ds(0, 48)], held.at[pl.ds(144, 48)], up, **to_up),
        send(corn.at[pl.ds(48, 48)], held.at[pl.ds(96, 48)], down, **to_down),
        send(cnt.at[1], cnt.at[2], up, **to_up),
        send(cnt.at[1], cnt.at[0], down, **to_down),
    ]

    gathers = []
    for step, offset, size in plan:
        own_at = pl.multiple_of(core * half + offset, 16)
        at = pl.multiple_of(dp * part + core * half + offset, 16)
        gathers.append(
            send(w_ref.at[pl.ds(own_at, size)], wfull.at[pl.ds(at, size)], along_z(step))
        )

    for copy in rows + second:
        copy.arrived()
    side_keys = dot(sides_ref[...], held[...])
    kall[pl.ds(SIDES, 96), :] = side_keys[:96].astype(BF)
    vall[pl.ds(SIDES, 96), :] = side_keys[96:].astype(BF)
    counts = dot(block_ref[...], cnt[...].reshape(96, 128).astype(BF))
    near = jnp.where(limit_ref[...].astype(F32) < counts, 0.0, NEG)
    bias[:, :TILES] = near
    bias[:, TILES:] = near

    lane = lax.broadcasted_iota(jnp.int32, (1, 128), 1)
    low = (lane < 64).astype(F32).astype(BF)
    high = (lane >= 64).astype(F32).astype(BF)

    def occupied(index):
        place = ((index >> 4) * 8 + (index & 7)).astype(F32)
        count = jnp.where(((index >> 3) & 1) == 0, count0, count1)
        return (place < count).astype(F32)

    valid_lane = occupied(lane)
    valid_row = occupied(lax.broadcasted_iota(jnp.int32, (TILES, CH), 0))

    def both(value):
        return jnp.concatenate([value * low, value * high], axis=0)

    def own_heads(value):
        return jnp.concatenate([value[:64, :TILES], value[64:, TILES:]], axis=0)

    def lanes(p):
        return pl.ds(pl.multiple_of(p * PAIR, PAIR), PAIR)

    @pl.loop(0, PAIRS)
    def _(p):
        keys, values = kall[:, lanes(p)], vall[:, lanes(p)]
        scores = dot(keys, both(q_ref[:, lanes(p)]), ((1,), (1,))) * HEAD_SCALE + bias[...]
        raised = jnp.exp(scores - jnp.max(scores, axis=0, keepdims=True))
        weights = raised * (1.0 / jnp.sum(raised, axis=0, keepdims=True))
        prob[p] = weights
        mixed = own_heads(dot(values, weights.astype(BF), ((0,), (0,))))
        attn_t[pl.ds(pl.multiple_of(p * PAIR, PAIR), PAIR), :] = (mixed * valid_lane).astype(BF)

    strip_rows = part // Y
    for d in range(DP):
        for j in range(Y):
            at = d * part + j * strip_rows
            term = dot(attn_t[pl.ds(at, strip_rows), :], go_ref[...])
            for c in range(2):
                piece = term[:, c * 384 : (c + 1) * 384]
                gw_own[c, j, d] = piece
                core_out[c, j, d] = piece.astype(BF)
    core_copy = send(core_out.at[1 - core], core_in, partner)

    passed = []
    for copy, (step, offset, size) in zip(gathers, plan):
        copy.arrived()
        source = (dp - step + DP) % DP
        at = pl.multiple_of(source * part + core * half + offset, 16)
        there = wfull.at[pl.ds(at, size)]
        passed.append(send(there, there, partner))
    for copy in passed:
        copy.arrived()
    back = dot(go_ref[...], wfull[...], ((1,), (1,))).astype(BF)
    gated[...] = back * valid_row.astype(BF)

    def backward(p):
        keys, values = kall[:, lanes(p)], vall[:, lanes(p)]
        queries, grads = both(q_ref[:, lanes(p)]), both(gated[:, lanes(p)])
        weights = prob[p]
        prob_grad = dot(values, grads, ((1,), (1,)))
        correction = jnp.sum(weights * prob_grad, axis=0, keepdims=True)
        score_grad = (weights * (prob_grad - correction) * HEAD_SCALE).astype(BF)
        key_part = dot(score_grad, queries)
        value_part = dot(weights.astype(BF), grads)
        dk_own[:, lanes(p)] = key_part[:TILES]
        dv_own[:, lanes(p)] = value_part[:TILES]
        row_out[0, :, lanes(p)] = key_part[UP:DOWN].astype(BF)
        row_out[1, :, lanes(p)] = value_part[UP:DOWN].astype(BF)
        row_out[2, :, lanes(p)] = key_part[DOWN:SIDES].astype(BF)
        row_out[3, :, lanes(p)] = value_part[DOWN:SIDES].astype(BF)
        dcol[pl.ds(0, 96), lanes(p)] = key_part[SIDES:].astype(BF)
        dcol[pl.ds(96, 96), lanes(p)] = value_part[SIDES:].astype(BF)
        query_part = own_heads(dot(keys, score_grad, ((0,), (0,))))
        dq_ref[:, lanes(p)] = query_part.T.astype(BF)

    pl.loop(0, PAIRS // 2)(backward)

    core_copy.arrived()
    total = gw_own[core] + core_in[...].astype(F32)
    y_sum[...] = total
    y_out[...] = total.astype(BF)
    y_copies = [
        send(y_out.at[(y + s) % Y], y_in.at[s - 1], along_y(s)) for s in range(1, Y)
    ]

    pl.loop(PAIRS // 2, PAIRS)(backward)

    bcorn[...] = dot(bcorn_ref[...], dcol[...]).astype(BF)
    back_corners = [
        send(bcorn.at[pl.ds(0, 48)], bcorn_in.at[pl.ds(48, 48)], up, **to_up),
        send(bcorn.at[pl.ds(48, 48)], bcorn_in.at[pl.ds(0, 48)], down, **to_down),
    ]
    back_rows = [
        send(row_out.at[pl.ds(0, 2)], row_in.at[pl.ds(2, 2)], up, **to_up),
        send(row_out.at[pl.ds(2, 2)], row_in.at[pl.ds(0, 2)], down, **to_down),
    ]

    for copy in back_corners:
        copy.arrived()
    returned = dot(bstrip_ref[:, :192], dcol[...]) + dot(bstrip_ref[:, 192:], bcorn_in[...])
    bstrip[...] = returned.astype(BF)
    back_strips = [
        send(bstrip.at[pl.ds(0, 48)], bstrip_in.at[pl.ds(48, 48)], left, **to_left),
        send(bstrip.at[pl.ds(48, 48)], bstrip_in.at[pl.ds(0, 48)], right, **to_right),
    ]

    for copy in y_copies:
        copy.arrived()
    total = y_sum[y]
    for s in range(1, Y):
        total = total + y_in[s - 1].astype(F32)
    x_sum[...] = total
    x_out[...] = total.astype(BF)
    x_copies = [
        send(x_out.at[(x + s) % X], x_in.at[s - 1], along_x(s)) for s in range(1, X)
    ]
    for copy in x_copies:
        copy.arrived()
    total = x_sum[x]
    for s in range(1, X):
        total = total + x_in[s - 1].astype(F32)
    z_out[...] = total.astype(BF)
    keeper = dp == x
    z_copies = []
    for s in range(1, DP):
        z_copies.append(
            send(z_out, z_in.at[s - 1], ((dp + s) % DP, row, col), sends=(dp + s) % DP == x, gets=keeper)
        )
    for copy in z_copies:
        copy.arrived()

    @pl.when(keeper)
    def _():
        gathered = total
        for s in range(1, DP):
            gathered = gathered + z_in[s - 1].astype(F32)
        h_all[zh] = gathered.astype(BF)

    h_copies = [
        send(h_all.at[zh], h_all.at[zh], along_hi(s), sends=keeper, gets=keeper)
        for s in range(1, ZH)
    ]
    for copy in h_copies:
        copy.arrived()

    @pl.when(keeper)
    def _():
        final = h_all[0].astype(F32)
        for s in range(1, ZH):
            final = final + h_all[s].astype(F32)
        g_all[core, y] = final.astype(BF)

    own_piece = g_all.at[core, y]
    spread = [
        send(own_piece, own_piece, along_x(s), sends=keeper, gets=(x + X - s) % X == dp)
        for s in range(1, X)
    ]
    for copy in spread:
        copy.arrived()
    spread_y = [send(own_piece, own_piece, along_y(s)) for s in range(1, Y)]

    for copy in back_rows + back_strips:
        copy.arrived()
    edge = bstrip_in[...]
    for kind, (own, out) in enumerate(((dk_own, dk_ref), (dv_own, dv_ref))):
        side_term = dot(unpack_ref[pl.ds(TILES * kind, TILES), :], edge)
        whole = own[...] + side_term
        top = whole[:48] + row_in[kind].astype(F32)
        bottom = whole[80:] + row_in[2 + kind].astype(F32)
        out[pl.ds(0, 48), :] = top.astype(BF)
        out[pl.ds(48, 32), :] = whole[48:80].astype(BF)
        out[pl.ds(80, 48), :] = bottom.astype(BF)

    for copy in spread_y:
        copy.arrived()
    core_back = send(g_all.at[core], g_all.at[core], partner)
    core_back.arrived()
    norm = (TILES * DP * ROWS * COLS) ** (-0.5)
    for c in range(2):
        for j in range(Y):
            gw_ref[pl.ds(j * strip_rows, strip_rows), pl.ds(c * 384, 384)] = (
                g_all[c, j].astype(F32) * norm
            )
    for copy in started:
        copy.sent()


COPIES = 64


def on_device(sizes, queries, keys, values, occupancy, out_weight, grad_out):
    DP, ROWS, COLS, X = sizes
    Y, ZH = ROWS // 2, COLS // X
    part = CH // DP
    strip_rows = part // Y
    flat = [a.reshape(TILES, CH) for a in (queries, keys, values, grad_out)]
    vmem = pl.BlockSpec(memory_space=pltpu.VMEM)
    piece = (strip_rows, 384)
    scratch = [
        pltpu.VMEM((KEYS, CH), BF),
        pltpu.VMEM((KEYS, CH), BF),
        pltpu.VMEM((96, CH), BF),
        pltpu.VMEM((192, CH), BF),
        pltpu.VMEM((96, CH), BF),
        pltpu.VMEM((3, 4, 8, 128), F32),
        pltpu.VMEM((CH, CH), BF),
        pltpu.VMEM((KEYS, 2 * TILES), F32),
        pltpu.VMEM((PAIRS, KEYS, 2 * TILES), F32),
        pltpu.VMEM((CH, TILES), BF),
        pltpu.VMEM((TILES, CH), BF),
        pltpu.VMEM((TILES, CH), F32),
        pltpu.VMEM((TILES, CH), F32),
        pltpu.VMEM((4, 48, CH), BF),
        pltpu.VMEM((4, 48, CH), BF),
        pltpu.VMEM((192, CH), BF),
        pltpu.VMEM((96, CH), BF),
        pltpu.VMEM((96, CH), BF),
        pltpu.VMEM((96, CH), BF),
        pltpu.VMEM((96, CH), BF),
        pltpu.VMEM((2, Y, DP) + piece, F32),
        pltpu.VMEM((2, Y, DP) + piece, BF),
        pltpu.VMEM((Y, DP) + piece, BF),
        pltpu.VMEM((Y, DP) + piece, F32),
        pltpu.VMEM((Y, DP) + piece, BF),
        pltpu.VMEM((max(Y - 1, 1), DP) + piece, BF),
        pltpu.VMEM((DP,) + piece, F32),
        pltpu.VMEM((DP,) + piece, BF),
        pltpu.VMEM((X - 1,) + piece, BF),
        pltpu.VMEM(piece, BF),
        pltpu.VMEM((DP - 1,) + piece, BF),
        pltpu.VMEM((ZH,) + piece, BF),
        pltpu.VMEM((2, Y) + piece, BF),
        pltpu.SemaphoreType.DMA((COPIES,)),
        pltpu.SemaphoreType.DMA((COPIES,)),
    ]
    tile_out = jax.ShapeDtypeStruct((TILES, CH), BF)
    grad_q, grad_k, grad_v, grad_w = pl.pallas_call(
        functools.partial(body, sizes),
        out_shape=(tile_out, tile_out, tile_out, jax.ShapeDtypeStruct((part, CH), F32)),
        in_specs=[vmem] * 5 + [pl.BlockSpec(memory_space=pltpu.SMEM)] + [vmem] * 8,
        out_specs=(vmem,) * 4,
        scratch_shapes=scratch,
        compiler_params=pltpu.CompilerParams(
            collective_id=0, has_side_effects=True, vmem_limit_bytes=50 * 2**20
        ),
        name="neighbourhood",
    )(*flat, out_weight, occupancy.reshape(1, 2), *(jnp.asarray(t) for t in tables()))
    shape = (1, HIGH, WIDE, CH)
    return grad_q.reshape(shape), grad_k.reshape(shape), grad_v.reshape(shape), grad_w


def solution(mesh):
    dp = mesh.shape["dp"]
    sizes = (dp, mesh.shape["row"], mesh.shape["col"], dp)
    tiles = P("dp", "row", "col", None)
    return jax.shard_map(
        functools.partial(on_device, sizes),
        mesh=mesh,
        in_specs=(tiles, tiles, tiles, P("dp", "row", "col"), P("dp", None), tiles),
        out_specs=(tiles, tiles, tiles, P("dp", None)),
        check_vma=False,
    )
```

time: 1020 us -> 93 us (0.09)
  the two profiles are of different devices: /device:TPU:46 before, /device:TPU:65 now
where the time goes in v1:
time: 93 us; the launch traced here: 92.3 us
  Pallas kernels  76.8 us (83%)
  local copies, waits for them, and re-layouts  14.9 us (16%)
    pallas_call x1, Pallas kernels, on_device(): pl.pallas_call(functools.partial(body, sizes), out_shape=(tile_out, tile_...  76.8 us
    unnamed x32, local copies, waits for them, and re-layouts  14.9 us

profile of v1, /device:TPU:65, one launch (start us, length us, event | category | flops | bytes accessed | tf_op | source)
XLA Modules:
  0.0 92.3 jit_solution(1566528141018379999)
XLA Ops:
  0.6 0.0 copy-start.13
  0.6 0.6 copy-done.13
  1.3 0.0 copy-start
  1.3 1.0 %copy-done = bf16[192,768]{1,0:T(8,128)(2,1)S(1)} copy-done((bf16[192,768]{1,0:T(8,128)(2,1)S(1)}, bf16[192,768]{1,0:T(8,128)(2,1)}, u32[]{:S(2)}) %copy-start) | copy-done | bytes 294936
  2.3 0.0 copy-start.1
  2.3 0.9 %copy-done.1 = bf16[1,8,16,768]{3,2,1,0:T(8,128)(2,1)S(1)} copy-done((bf16[1,8,16,768]{3,2,1,0:T(8,128)(2,1)S(1)}, bf16[1,8,16,768]{3,2,1,0:T(8,128)(2,1)}, u32[]{:S(2)}) %copy-start.1) | copy-done | bytes 196632
  3.2 0.0 copy-start.2
  3.2 0.9 %copy-done.2 = bf16[1,8,16,768]{3,2,1,0:T(8,128)(2,1)S(1)} copy-done((bf16[1,8,16,768]{3,2,1,0:T(8,128)(2,1)S(1)}, bf16[1,8,16,768]{3,2,1,0:T(8,128)(2,1)}, u32[]{:S(2)}) %copy-start.2) | copy-done | bytes 196632
  4.1 0.0 copy-start.3
  4.1 0.9 %copy-done.3 = bf16[1,8,16,768]{3,2,1,0:T(8,128)(2,1)S(1)} copy-done((bf16[1,8,16,768]{3,2,1,0:T(8,128)(2,1)S(1)}, bf16[1,8,16,768]{3,2,1,0:T(8,128)(2,1)}, u32[]{:S(2)}) %copy-start.3) | copy-done | bytes 196632
  5.0 0.9 %copy-done.4 = bf16[1,8,16,768]{3,2,1,0:T(8,128)(2,1)S(1)} copy-done((bf16[1,8,16,768]{3,2,1,0:T(8,128)(2,1)S(1)}, bf16[1,8,16,768]{3,2,1,0:T(8,128)(2,1)}, u32[]{:S(2)}) %copy-start.4) | copy-done | bytes 196632
  6.0 0.9 copy-done.5
  6.9 0.9 copy-done.6
  7.7 0.9 copy-done.7
  8.6 0.9 copy-done.8
  9.5 0.8 copy-done.9
  10.4 0.8 copy-done.10
  11.2 0.8 copy-done.11
  12.0 0.7 copy-done.12
  12.7 76.8 %neighbourhood.1 = (bf16[128,768]{1,0:T(8,128)(2,1)S(1)}, bf16[128,768]{1,0:T(8,128)(2,1)S(1)}, bf16[128,768]{1,0:T(8,128)(2,1)S(1)}, f32[192,768]{1,0:T(8,128)S(1)}) custom-call(bf16[128,768]{1,0:T(8,128)(2,1)S(1)} %bitcast.11, bf16[128,768]{1,0:T(8,128)(2,1)S(1)} %bitcast.12, bf16[128,768]{1,0:T(8,128)(2,1)S(1)} %bitcast.13, ...), custom_call_target="tpu_custom_call" | custom-call | tf_op jit(solution)/shard_map/neighbourhood/pallas_call | solution.py:491
  89.5 0.7 copy.22
  90.2 0.7 copy.23
  90.9 0.7 copy.24
  91.5 0.8 copy.25
  (9 shorter events, 0.0 us)
Async XLA Ops:
  0.6 0.7 copy-start.13
  1.3 1.0 %copy-start = (bf16[192,768]{1,0:T(8,128)(2,1)S(1)}, bf16[192,768]{1,0:T(8,128)(2,1)}, u32[]{:S(2)}) copy-start(bf16[192,768]{1,0:T(8,128)(2,1)} %w_ref.1) | copy-start | bytes 884740
  2.3 0.9 %copy-start.1 = (bf16[1,8,16,768]{3,2,1,0:T(8,128)(2,1)S(1)}, bf16[1,8,16,768]{3,2,1,0:T(8,128)(2,1)}, u32[]{:S(2)}) copy-start(bf16[1,8,16,768]{3,2,1,0:T(8,128)(2,1)} %param.14) | copy-start | bytes 589828
  3.2 0.9 %copy-start.2 = (bf16[1,8,16,768]{3,2,1,0:T(8,128)(2,1)S(1)}, bf16[1,8,16,768]{3,2,1,0:T(8,128)(2,1)}, u32[]{:S(2)}) copy-start(bf16[1,8,16,768]{3,2,1,0:T(8,128)(2,1)} %param.15) | copy-start | bytes 589828
  4.1 0.9 %copy-start.3 = (bf16[1,8,16,768]{3,2,1,0:T(8,128)(2,1)S(1)}, bf16[1,8,16,768]{3,2,1,0:T(8,128)(2,1)}, u32[]{:S(2)}) copy-start(bf16[1,8,16,768]{3,2,1,0:T(8,128)(2,1)} %param.16) | copy-start | bytes 589828
  5.0 0.9 %copy-start.4 = (bf16[1,8,16,768]{3,2,1,0:T(8,128)(2,1)S(1)}, bf16[1,8,16,768]{3,2,1,0:T(8,128)(2,1)}, u32[]{:S(2)}) copy-start(bf16[1,8,16,768]{3,2,1,0:T(8,128)(2,1)} %param.19) | copy-start | bytes 589828
  6.0 0.9 copy-start.5
  6.9 0.9 copy-start.6
  7.7 0.9 copy-start.7
  8.6 0.9 copy-start.8
  9.5 0.8 copy-start.9
  10.4 0.8 copy-start.10
  11.2 0.8 copy-start.11
  12.0 0.7 copy-start.12

commit v2 on v1

--- a/solution.py
+++ b/solution.py
@@ -92,13 +92,15 @@
 
 def body(
     sizes,
-    q_ref, k_ref, v_ref, go_ref, w_ref, occ_ref,
+    q_in, k_in, v_in, go_in, w_in, occ_in,
+    limit_in, block_in, pack_in, corners_in, sides_in, bcorn_in_, bstrip_in_, unpack_in,
+    dq_ref, dk_ref, dv_ref, gw_ref,
+    q_ref, go_ref, w_ref, occ_ref,
     limit_ref, block_ref, pack_ref, corners_ref, sides_ref, bcorn_ref, bstrip_ref, unpack_ref,
-    dq_ref, dk_ref, dv_ref, gw_ref,
     kall, vall, strips, held, corn, cnt, wfull, bias, prob, attn_t, gated,
     dk_own, dv_own, row_out, row_in, dcol, bcorn, bcorn_in, bstrip, bstrip_in,
     gw_own, core_out, core_in, y_sum, y_out, y_in, x_sum, x_out, x_in, z_out, z_in, h_all, g_all,
-    ssem, rsem,
+    ssem, rsem, lsem, far,
 ):
     DP, ROWS, COLS, X = sizes
     Y, ZH = ROWS // 2, COLS // X
@@ -136,6 +138,19 @@
     else:
         plan = [(1, 0, half // 2), (-1, half // 2, half // 2)]
 
+    own = pl.ds(0, TILES)
+    loads = [
+        (occ_in, occ_ref), (pack_in, pack_ref), (k_in, kall.at[own]), (v_in, vall.at[own]),
+        (corners_in, corners_ref), (w_in, w_ref), (sides_in, sides_ref), (block_in, block_ref),
+        (limit_in, limit_ref), (q_in, q_ref), (go_in, go_ref), (bcorn_in_, bcorn_ref),
+        (bstrip_in_, bstrip_ref), (unpack_in, unpack_ref),
+    ]
+    loads = [
+        pltpu.make_async_copy(src, dst, lsem.at[i]) for i, (src, dst) in enumerate(loads)
+    ]
+    for load in loads:
+        load.start()
+
     kall[pl.ds(UP, 96), :] = jnp.zeros((96, CH), BF)
     vall[pl.ds(UP, 96), :] = jnp.zeros((96, CH), BF)
     held[...] = jnp.zeros(held.shape, BF)
@@ -153,14 +168,15 @@
         pl.when(there)(functools.partial(greet, device))
     fixed = [partner] + [along_z(step) for step, _, _ in plan]
     fixed += [along_y(s) for s in range(1, Y)] + [along_x(s) for s in range(1, X)]
-    fixed += [along_lo(s) for s in range(1, DP)] + [along_hi(s) for s in range(1, ZH)]
     for device in fixed:
         greet(device)
 
+    for load in loads[:4]:
+        load.wait()
     count0, count1 = occ_ref[0, 0].astype(F32), occ_ref[0, 1].astype(F32)
     cnt[1, 1] = jnp.full((8, 128), count0, F32)
     cnt[1, 2] = jnp.full((8, 128), count1, F32)
-    packed = dot(pack_ref[:, :TILES], k_ref[...]) + dot(pack_ref[:, TILES:], v_ref[...])
+    packed = dot(pack_ref[:, :TILES], kall[own, :]) + dot(pack_ref[:, TILES:], vall[own, :])
     strips[...] = packed.astype(BF)
 
     around = sum(t.astype(jnp.int32) for t in (has_up, has_down, has_left, has_right))
@@ -215,13 +231,13 @@
         send(strips.at[pl.ds(48, 48)], held.at[pl.ds(0, 48)], right, **to_right),
     ]
     rows = [
-        send(k_ref.at[pl.ds(0, 48)], kall.at[pl.ds(DOWN, 48)], up, **to_up),
-        send(k_ref.at[pl.ds(80, 48)], kall.at[pl.ds(UP, 48)], down, **to_down),
-        send(v_ref.at[pl.ds(0, 48)], vall.at[pl.ds(DOWN, 48)], up, **to_up),
-        send(v_ref.at[pl.ds(80, 48)], vall.at[pl.ds(UP, 48)], down, **to_down),
-    ]
-    kall[pl.ds(0, TILES), :] = k_ref[...]
-    vall[pl.ds(0, TILES), :] = v_ref[...]
+        send(kall.at[pl.ds(0, 48)], kall.at[pl.ds(DOWN, 48)], up, **to_up),
+        send(kall.at[pl.ds(80, 48)], kall.at[pl.ds(UP, 48)], down, **to_down),
+        send(vall.at[pl.ds(0, 48)], vall.at[pl.ds(DOWN, 48)], up, **to_up),
+        send(vall.at[pl.ds(80, 48)], vall.at[pl.ds(UP, 48)], down, **to_down),
+    ]
+    for load in loads[4:]:
+        load.wait()
     base = pl.multiple_of(dp * part, 16)
     wfull[pl.ds(base, part), :] = w_ref[...]
 
@@ -302,10 +318,19 @@
         at = pl.multiple_of(source * part + core * half + offset, 16)
         there = wfull.at[pl.ds(at, size)]
         passed.append(send(there, there, partner))
+    pl.semaphore_signal(far, inc=1, device_id=along_hi(1), device_id_type=MESH)
     for copy in passed:
         copy.arrived()
     back = dot(go_ref[...], wfull[...], ((1,), (1,))).astype(BF)
     gated[...] = back * valid_row.astype(BF)
+
+    core_copy.arrived()
+    total = gw_own[core] + core_in[...].astype(F32)
+    y_sum[...] = total
+    y_out[...] = total.astype(BF)
+    y_copies = [
+        send(y_out.at[(y + s) % Y], y_in.at[s - 1], along_y(s)) for s in range(1, Y)
+    ]
 
     def backward(p):
         keys, values = kall[:, lanes(p)], vall[:, lanes(p)]
@@ -327,36 +352,7 @@
         query_part = own_heads(dot(keys, score_grad, ((0,), (0,))))
         dq_ref[:, lanes(p)] = query_part.T.astype(BF)
 
-    pl.loop(0, PAIRS // 2)(backward)
-
-    core_copy.arrived()
-    total = gw_own[core] + core_in[...].astype(F32)
-    y_sum[...] = total
-    y_out[...] = total.astype(BF)
-    y_copies = [
-        send(y_out.at[(y + s) % Y], y_in.at[s - 1], along_y(s)) for s in range(1, Y)
-    ]
-
-    pl.loop(PAIRS // 2, PAIRS)(backward)
-
-    bcorn[...] = dot(bcorn_ref[...], dcol[...]).astype(BF)
-    back_corners = [
-        send(bcorn.at[pl.ds(0, 48)], bcorn_in.at[pl.ds(48, 48)], up, **to_up),
-        send(bcorn.at[pl.ds(48, 48)], bcorn_in.at[pl.ds(0, 48)], down, **to_down),
-    ]
-    back_rows = [
-        send(row_out.at[pl.ds(0, 2)], row_in.at[pl.ds(2, 2)], up, **to_up),
-        send(row_out.at[pl.ds(2, 2)], row_in.at[pl.ds(0, 2)], down, **to_down),
-    ]
-
-    for copy in back_corners:
-        copy.arrived()
-    returned = dot(bstrip_ref[:, :192], dcol[...]) + dot(bstrip_ref[:, 192:], bcorn_in[...])
-    bstrip[...] = returned.astype(BF)
-    back_strips = [
-        send(bstrip.at[pl.ds(0, 48)], bstrip_in.at[pl.ds(48, 48)], left, **to_left),
-        send(bstrip.at[pl.ds(48, 48)], bstrip_in.at[pl.ds(0, 48)], right, **to_right),
-    ]
+    pl.loop(0, 4)(backward)
 
     for copy in y_copies:
         copy.arrived()
@@ -368,6 +364,19 @@
     x_copies = [
         send(x_out.at[(x + s) % X], x_in.at[s - 1], along_x(s)) for s in range(1, X)
     ]
+
+    pl.loop(4, PAIRS)(backward)
+
+    bcorn[...] = dot(bcorn_ref[...], dcol[...]).astype(BF)
+    back_corners = [
+        send(bcorn.at[pl.ds(0, 48)], bcorn_in.at[pl.ds(48, 48)], up, **to_up),
+        send(bcorn.at[pl.ds(48, 48)], bcorn_in.at[pl.ds(0, 48)], down, **to_down),
+    ]
+    back_rows = [
+        send(row_out.at[pl.ds(0, 2)], row_in.at[pl.ds(2, 2)], up, **to_up),
+        send(row_out.at[pl.ds(2, 2)], row_in.at[pl.ds(0, 2)], down, **to_down),
+    ]
+
     for copy in x_copies:
         copy.arrived()
     total = x_sum[x]
@@ -380,6 +389,16 @@
         z_copies.append(
             send(z_out, z_in.at[s - 1], ((dp + s) % DP, row, col), sends=(dp + s) % DP == x, gets=keeper)
         )
+
+    for copy in back_corners:
+        copy.arrived()
+    returned = dot(bstrip_ref[:, :192], dcol[...]) + dot(bstrip_ref[:, 192:], bcorn_in[...])
+    bstrip[...] = returned.astype(BF)
+    back_strips = [
+        send(bstrip.at[pl.ds(0, 48)], bstrip_in.at[pl.ds(48, 48)], left, **to_left),
+        send(bstrip.at[pl.ds(48, 48)], bstrip_in.at[pl.ds(0, 48)], right, **to_right),
+    ]
+
     for copy in z_copies:
         copy.arrived()
 
@@ -390,29 +409,11 @@
             gathered = gathered + z_in[s - 1].astype(F32)
         h_all[zh] = gathered.astype(BF)
 
+    pl.semaphore_wait(far, 1)
     h_copies = [
         send(h_all.at[zh], h_all.at[zh], along_hi(s), sends=keeper, gets=keeper)
         for s in range(1, ZH)
     ]
-    for copy in h_copies:
-        copy.arrived()
-
-    @pl.when(keeper)
-    def _():
-        final = h_all[0].astype(F32)
-        for s in range(1, ZH):
-            final = final + h_all[s].astype(F32)
-        g_all[core, y] = final.astype(BF)
-
-    own_piece = g_all.at[core, y]
-    spread = [
-        send(own_piece, own_piece, along_x(s), sends=keeper, gets=(x + X - s) % X == dp)
-        for s in range(1, X)
-    ]
-    for copy in spread:
-        copy.arrived()
-    spread_y = [send(own_piece, own_piece, along_y(s)) for s in range(1, Y)]
-
     for copy in back_rows + back_strips:
         copy.arrived()
     edge = bstrip_in[...]
@@ -424,6 +425,25 @@
         out[pl.ds(0, 48), :] = top.astype(BF)
         out[pl.ds(48, 32), :] = whole[48:80].astype(BF)
         out[pl.ds(80, 48), :] = bottom.astype(BF)
+
+    for copy in h_copies:
+        copy.arrived()
+
+    @pl.when(keeper)
+    def _():
+        final = h_all[0].astype(F32)
+        for s in range(1, ZH):
+            final = final + h_all[s].astype(F32)
+        g_all[core, y] = final.astype(BF)
+
+    own_piece = g_all.at[core, y]
+    spread = [
+        send(own_piece, own_piece, along_x(s), sends=keeper, gets=(x + X - s) % X == dp)
+        for s in range(1, X)
+    ]
+    for copy in spread:
+        copy.arrived()
+    spread_y = [send(own_piece, own_piece, along_y(s)) for s in range(1, Y)]
 
     for copy in spread_y:
         copy.arrived()
@@ -449,8 +469,15 @@
     strip_rows = part // Y
     flat = [a.reshape(TILES, CH) for a in (queries, keys, values, grad_out)]
     vmem = pl.BlockSpec(memory_space=pltpu.VMEM)
+    hbm = pl.BlockSpec(memory_space=pltpu.HBM)
+    fixed = tables()
     piece = (strip_rows, 384)
     scratch = [
+        pltpu.VMEM((TILES, CH), BF),
+        pltpu.VMEM((TILES, CH), BF),
+        pltpu.VMEM((part, CH), BF),
+        pltpu.SMEM((1, 2), jnp.int32),
+        *(pltpu.VMEM(t.shape, BF) for t in fixed),
         pltpu.VMEM((KEYS, CH), BF),
         pltpu.VMEM((KEYS, CH), BF),
         pltpu.VMEM((96, CH), BF),
@@ -486,19 +513,21 @@
         pltpu.VMEM((2, Y) + piece, BF),
         pltpu.SemaphoreType.DMA((COPIES,)),
         pltpu.SemaphoreType.DMA((COPIES,)),
+        pltpu.SemaphoreType.DMA((14,)),
+        pltpu.SemaphoreType.REGULAR,
     ]
     tile_out = jax.ShapeDtypeStruct((TILES, CH), BF)
     grad_q, grad_k, grad_v, grad_w = pl.pallas_call(
         functools.partial(body, sizes),
         out_shape=(tile_out, tile_out, tile_out, jax.ShapeDtypeStruct((part, CH), F32)),
-        in_specs=[vmem] * 5 + [pl.BlockSpec(memory_space=pltpu.SMEM)] + [vmem] * 8,
+        in_specs=[hbm] * 14,
         out_specs=(vmem,) * 4,
         scratch_shapes=scratch,
         compiler_params=pltpu.CompilerParams(
-            collective_id=0, has_side_effects=True, vmem_limit_bytes=50 * 2**20
+            collective_id=0, has_side_effects=True, vmem_limit_bytes=67043328
         ),
         name="neighbourhood",
-    )(*flat, out_weight, occupancy.reshape(1, 2), *(jnp.asarray(t) for t in tables()))
+    )(*flat, out_weight, occupancy.reshape(1, 2), *(jnp.asarray(t) for t in fixed))
     shape = (1, HIGH, WIDE, CH)
     return grad_q.reshape(shape), grad_k.reshape(shape), grad_v.reshape(shape), grad_w
 

time: 93 us -> 78.5 us (0.84)
  the two profiles are of different devices: /device:TPU:65 before, /device:TPU:5 now
where the time goes in v2:
time: 78.5 us; the launch traced here: 78.3 us
  Pallas kernels  72.8 us (93%)
  local copies, waits for them, and re-layouts  4.83 us (6%)
    pallas_call x1, Pallas kernels, on_device(): pl.pallas_call(functools.partial(body, sizes), out_shape=(tile_out, tile_...  72.8 us
    unnamed x8, local copies, waits for them, and re-layouts  4.83 us

profile of v2, /device:TPU:5, one launch (start us, length us, event | category | flops | bytes accessed | tf_op | source)
XLA Modules:
  0.0 78.3 jit_solution(8579582406943183648)
XLA Ops:
  0.6 72.8 %neighbourhood.1 = (bf16[128,768]{1,0:T(8,128)(2,1)}, bf16[128,768]{1,0:T(8,128)(2,1)}, bf16[128,768]{1,0:T(8,128)(2,1)}, f32[192,768]{1,0:T(8,128)}) custom-call(bf16[128,768]{1,0:T(8,128)(2,1)} %bitcast.11, bf16[128,768]{1,0:T(8,128)(2,1)} %bitcast.12, bf16[128,768]{1,0:T(8,128)(2,1)} %bitcast.13, bf16[128,768]{1,0:T(8,128)(2,1)} %bitcast.14, ...), custom_call_target="tpu_custom_call" | custom-call | tf_op jit(solution)/shard_map/neighbourhood/pallas_call | solution.py:520
  73.5 0.0 copy-start
  73.5 1.7 %copy.22 = bf16[1,8,16,768]{3,2,1,0:T(8,128)(2,1)} copy(bf16[1,8,16,768]{3,2,1,0:T(8,128)(2,1)} %bitcast.10) | data formatting | bytes 393216
  75.2 0.0 copy-start.1
  75.2 1.7 %copy.23 = bf16[1,8,16,768]{3,2,1,0:T(8,128)(2,1)} copy(bf16[1,8,16,768]{3,2,1,0:T(8,128)(2,1)} %bitcast.9) | data formatting | bytes 393216
  76.8 0.0 copy-done.1
  76.8 0.7 copy.24
  77.5 0.0 copy-done
  77.5 0.8 %copy.25 = f32[192,768]{1,0:T(8,128)} copy(f32[192,768]{1,0:T(8,128)S(1)} %copy-done) | data formatting | bytes 1179648
Async XLA Ops:
  73.5 4.0 %copy-start = (f32[192,768]{1,0:T(8,128)S(1)}, f32[192,768]{1,0:T(8,128)}, u32[]{:S(2)}) copy-start(f32[192,768]{1,0:T(8,128)} %get-tuple-element.19) | copy-start | bytes 1769476
  75.2 1.7 %copy-start.1 = (bf16[128,768]{1,0:T(8,128)(2,1)S(1)}, bf16[128,768]{1,0:T(8,128)(2,1)}, u32[]{:S(2)}) copy-start(bf16[128,768]{1,0:T(8,128)(2,1)} %get-tuple-element.10) | copy-start | bytes 589828

commit v3 on v2

--- a/solution.py
+++ b/solution.py
@@ -99,7 +99,7 @@
     limit_ref, block_ref, pack_ref, corners_ref, sides_ref, bcorn_ref, bstrip_ref, unpack_ref,
     kall, vall, strips, held, corn, cnt, wfull, bias, prob, attn_t, gated,
     dk_own, dv_own, row_out, row_in, dcol, bcorn, bcorn_in, bstrip, bstrip_in,
-    gw_own, core_out, core_in, y_sum, y_out, y_in, x_sum, x_out, x_in, z_out, z_in, h_all, g_all,
+    gw_own, core_out, core_in, xy_sum, y_out, y_in, x_out, x_in, half_sum, half_out, e_in, z_out, z_in, h_all, g_all,
     ssem, rsem, lsem, far,
 ):
     DP, ROWS, COLS, X = sizes
@@ -288,10 +288,11 @@
         return jnp.concatenate([value[:64, :TILES], value[64:, TILES:]], axis=0)
 
     def lanes(p):
+        if isinstance(p, int):
+            return pl.ds(p * PAIR, PAIR)
         return pl.ds(pl.multiple_of(p * PAIR, PAIR), PAIR)
 
-    @pl.loop(0, PAIRS)
-    def _(p):
+    def forward(p):
         keys, values = kall[:, lanes(p)], vall[:, lanes(p)]
         scores = dot(keys, both(q_ref[:, lanes(p)]), ((1,), (1,))) * HEAD_SCALE + bias[...]
         raised = jnp.exp(scores - jnp.max(scores, axis=0, keepdims=True))
@@ -301,15 +302,46 @@
         attn_t[pl.ds(pl.multiple_of(p * PAIR, PAIR), PAIR), :] = (mixed * valid_lane).astype(BF)
 
     strip_rows = part // Y
-    for d in range(DP):
+
+    def term_of(h, which):
+        columns = pl.ds(pl.multiple_of(which * 384, 128), 384)
+        return dot(attn_t[pl.ds(384 * h, 384), :], go_ref[:, columns])
+
+    def cut(term, i, j):
+        return term[i * part + j * strip_rows :][:strip_rows]
+
+    core_copies = []
+    for h in range(2):
+        pl.loop(3 * h, 3 * h + 3)(forward)
+        term = term_of(h, 1 - core)
         for j in range(Y):
-            at = d * part + j * strip_rows
-            term = dot(attn_t[pl.ds(at, strip_rows), :], go_ref[...])
-            for c in range(2):
-                piece = term[:, c * 384 : (c + 1) * 384]
-                gw_own[c, j, d] = piece
-                core_out[c, j, d] = piece.astype(BF)
-    core_copy = send(core_out.at[1 - core], core_in, partner)
+            for i in range(2):
+                core_out[h, j, i] = cut(term, i, j).astype(BF)
+        core_copies.append(send(core_out.at[h], core_in.at[h], partner))
+        term = term_of(h, core)
+        for j in range(Y):
+            for i in range(2):
+                gw_own[h, j, i] = cut(term, i, j)
+
+    y_copies, x_copies = [], []
+    for h in range(2):
+        core_copies[h].arrived()
+        for j in range(Y):
+            for i in range(2):
+                d = 2 * h + i
+                total = gw_own[h, j, i] + core_in[h, j, i].astype(F32)
+                xy_sum[j, d] = total
+                if (d + j) % 2 == 0:
+                    y_out[h, j] = total.astype(BF)
+                else:
+                    x_out[d, j // 2] = total.astype(BF)
+        for s in range(1, Y):
+            y_copies.append(send(y_out.at[h, (y + s) % Y], y_in.at[s - 1, h], along_y(s)))
+        for s in range(1, X):
+            there = (x + s) % X
+            x_copies.append(
+                send(x_out.at[there], x_in.at[s - 1], along_x(s), sends=there // 2 == h, gets=x // 2 == h)
+            )
 
     passed = []
     for copy, (step, offset, size) in zip(gathers, plan):
@@ -323,14 +355,6 @@
         copy.arrived()
     back = dot(go_ref[...], wfull[...], ((1,), (1,))).astype(BF)
     gated[...] = back * valid_row.astype(BF)
-
-    core_copy.arrived()
-    total = gw_own[core] + core_in[...].astype(F32)
-    y_sum[...] = total
-    y_out[...] = total.astype(BF)
-    y_copies = [
-        send(y_out.at[(y + s) % Y], y_in.at[s - 1], along_y(s)) for s in range(1, Y)
-    ]
 
     def backward(p):
         keys, values = kall[:, lanes(p)], vall[:, lanes(p)]
@@ -352,36 +376,46 @@
         query_part = own_heads(dot(keys, score_grad, ((0,), (0,))))
         dq_ref[:, lanes(p)] = query_part.T.astype(BF)
 
-    pl.loop(0, 4)(backward)
-
-    for copy in y_copies:
-        copy.arrived()
-    total = y_sum[y]
+    def run(first, last):
+        if UNROLLED:
+            for p in range(first, last):
+                backward(p)
+        else:
+            pl.loop(first, last)(backward)
+
+    run(0, 2)
+    for copy in y_copies + x_copies:
+        copy.arrived()
+    for i in range(2):
+        total = xy_sum[y, 2 * i + y % 2]
+        for s in range(1, Y):
+            total = total + y_in[s - 1, i].astype(F32)
+        half_sum[i] = total
+        half_out[i] = total.astype(BF)
+        total = xy_sum[2 * i + (x + 1) % 2, x]
+        for s in range(1, X):
+            total = total + x_in[s - 1, i].astype(F32)
+        half_sum[2 + i] = total
+        half_out[2 + i] = total.astype(BF)
+    odd = (x + y) % 2
+    second_copies = []
+    for s in range(1, X):
+        there = (x + s) % X
+        second_copies.append(
+            send(half_out.at[there // 2], e_in.at[s - 1], along_x(s), sends=(there + y) % 2 == 0, gets=odd == 0)
+        )
     for s in range(1, Y):
-        total = total + y_in[s - 1].astype(F32)
-    x_sum[...] = total
-    x_out[...] = total.astype(BF)
-    x_copies = [
-        send(x_out.at[(x + s) % X], x_in.at[s - 1], along_x(s)) for s in range(1, X)
-    ]
-
-    pl.loop(4, PAIRS)(backward)
-
-    bcorn[...] = dot(bcorn_ref[...], dcol[...]).astype(BF)
-    back_corners = [
-        send(bcorn.at[pl.ds(0, 48)], bcorn_in.at[pl.ds(48, 48)], up, **to_up),
-        send(bcorn.at[pl.ds(48, 48)], bcorn_in.at[pl.ds(0, 48)], down, **to_down),
-    ]
-    back_rows = [
-        send(row_out.at[pl.ds(0, 2)], row_in.at[pl.ds(2, 2)], up, **to_up),
-        send(row_out.at[pl.ds(2, 2)], row_in.at[pl.ds(0, 2)], down, **to_down),
-    ]
-
-    for copy in x_copies:
-        copy.arrived()
-    total = x_sum[x]
+        there = (y + s) % Y
+        second_copies.append(
+            send(half_out.at[2 + there // 2], e_in.at[s - 1], along_y(s), sends=(there + x) % 2 == 1, gets=odd == 1)
+        )
+
+    run(2, 5)
+    for copy in second_copies:
+        copy.arrived()
+    total = half_sum[odd * (2 + y // 2) + (1 - odd) * (x // 2)]
     for s in range(1, X):
-        total = total + x_in[s - 1].astype(F32)
+        total = total + e_in[s - 1].astype(F32)
     z_out[...] = total.astype(BF)
     keeper = dp == x
     z_copies = []
@@ -390,13 +424,15 @@
             send(z_out, z_in.at[s - 1], ((dp + s) % DP, row, col), sends=(dp + s) % DP == x, gets=keeper)
         )
 
-    for copy in back_corners:
-        copy.arrived()
-    returned = dot(bstrip_ref[:, :192], dcol[...]) + dot(bstrip_ref[:, 192:], bcorn_in[...])
-    bstrip[...] = returned.astype(BF)
-    back_strips = [
-        send(bstrip.at[pl.ds(0, 48)], bstrip_in.at[pl.ds(48, 48)], left, **to_left),
-        send(bstrip.at[pl.ds(48, 48)], bstrip_in.at[pl.ds(0, 48)], right, **to_right),
+    run(5, 6)
+    bcorn[...] = dot(bcorn_ref[...], dcol[...]).astype(BF)
+    back_corners = [
+        send(bcorn.at[pl.ds(0, 48)], bcorn_in.at[pl.ds(48, 48)], up, **to_up),
+        send(bcorn.at[pl.ds(48, 48)], bcorn_in.at[pl.ds(0, 48)], down, **to_down),
+    ]
+    back_rows = [
+        send(row_out.at[pl.ds(0, 2)], row_in.at[pl.ds(2, 2)], up, **to_up),
+        send(row_out.at[pl.ds(2, 2)], row_in.at[pl.ds(0, 2)], down, **to_down),
     ]
 
     for copy in z_copies:
@@ -414,17 +450,14 @@
         send(h_all.at[zh], h_all.at[zh], along_hi(s), sends=keeper, gets=keeper)
         for s in range(1, ZH)
     ]
-    for copy in back_rows + back_strips:
-        copy.arrived()
-    edge = bstrip_in[...]
-    for kind, (own, out) in enumerate(((dk_own, dk_ref), (dv_own, dv_ref))):
-        side_term = dot(unpack_ref[pl.ds(TILES * kind, TILES), :], edge)
-        whole = own[...] + side_term
-        top = whole[:48] + row_in[kind].astype(F32)
-        bottom = whole[80:] + row_in[2 + kind].astype(F32)
-        out[pl.ds(0, 48), :] = top.astype(BF)
-        out[pl.ds(48, 32), :] = whole[48:80].astype(BF)
-        out[pl.ds(80, 48), :] = bottom.astype(BF)
+    for copy in back_corners:
+        copy.arrived()
+    returned = dot(bstrip_ref[:, :192], dcol[...]) + dot(bstrip_ref[:, 192:], bcorn_in[...])
+    bstrip[...] = returned.astype(BF)
+    back_strips = [
+        send(bstrip.at[pl.ds(0, 48)], bstrip_in.at[pl.ds(48, 48)], left, **to_left),
+        send(bstrip.at[pl.ds(48, 48)], bstrip_in.at[pl.ds(0, 48)], right, **to_right),
+    ]
 
     for copy in h_copies:
         copy.arrived()
@@ -441,9 +474,22 @@
         send(own_piece, own_piece, along_x(s), sends=keeper, gets=(x + X - s) % X == dp)
         for s in range(1, X)
     ]
+    for copy in back_rows:
+        copy.arrived()
+    for kind, total in enumerate((dk_own, dv_own)):
+        total[pl.ds(0, 48), :] += row_in[kind].astype(F32)
+        total[pl.ds(80, 48), :] += row_in[2 + kind].astype(F32)
+
     for copy in spread:
         copy.arrived()
     spread_y = [send(own_piece, own_piece, along_y(s)) for s in range(1, Y)]
+
+    for copy in back_strips:
+        copy.arrived()
+    edge = bstrip_in[...]
+    for kind, (total, out) in enumerate(((dk_own, dk_ref), (dv_own, dv_ref))):
+        side_term = dot(unpack_ref[pl.ds(TILES * kind, TILES), :], edge)
+        out[...] = (total[...] + side_term).astype(BF)
 
     for copy in spread_y:
         copy.arrived()
@@ -460,6 +506,21 @@
 
 
 COPIES = 64
+UNROLLED = False
+LIMIT = 67043328
+
+
+def deliver(*refs):
+    sources, targets, held, into, out = refs[:4], refs[4:8], refs[8:12], refs[12], refs[13]
+    first = [pltpu.make_async_copy(s, h, into.at[i]) for i, (s, h) in enumerate(zip(sources, held))]
+    then = [pltpu.make_async_copy(h, t, out.at[i]) for i, (h, t) in enumerate(zip(held, targets))]
+    for copy in first:
+        copy.start()
+    for copy, following in zip(first, then):
+        copy.wait()
+        following.start()
+    for copy in then:
+        copy.wait()
 
 
 def on_device(sizes, queries, keys, values, occupancy, out_weight, grad_out):
@@ -498,15 +559,17 @@
         pltpu.VMEM((96, CH), BF),
         pltpu.VMEM((96, CH), BF),
         pltpu.VMEM((96, CH), BF),
-        pltpu.VMEM((2, Y, DP) + piece, F32),
-        pltpu.VMEM((2, Y, DP) + piece, BF),
-        pltpu.VMEM((Y, DP) + piece, BF),
+        pltpu.VMEM((2, Y, 2) + piece, F32),
+        pltpu.VMEM((2, Y, 2) + piece, BF),
+        pltpu.VMEM((2, Y, 2) + piece, BF),
         pltpu.VMEM((Y, DP) + piece, F32),
-        pltpu.VMEM((Y, DP) + piece, BF),
-        pltpu.VMEM((max(Y - 1, 1), DP) + piece, BF),
-        pltpu.VMEM((DP,) + piece, F32),
-        pltpu.VMEM((DP,) + piece, BF),
-        pltpu.VMEM((X - 1,) + piece, BF),
+        pltpu.VMEM((2, Y) + piece, BF),
+        pltpu.VMEM((Y - 1, DP // 2) + piece, BF),
+        pltpu.VMEM((DP, Y // 2) + piece, BF),
+        pltpu.VMEM((X - 1, Y // 2) + piece, BF),
+        pltpu.VMEM((4,) + piece, F32),
+        pltpu.VMEM((4,) + piece, BF),
+        pltpu.VMEM((3,) + piece, BF),
         pltpu.VMEM(piece, BF),
         pltpu.VMEM((DP - 1,) + piece, BF),
         pltpu.VMEM((ZH,) + piece, BF),
@@ -517,17 +580,28 @@
         pltpu.SemaphoreType.REGULAR,
     ]
     tile_out = jax.ShapeDtypeStruct((TILES, CH), BF)
-    grad_q, grad_k, grad_v, grad_w = pl.pallas_call(
+    outs = (tile_out, tile_out, tile_out, jax.ShapeDtypeStruct((part, CH), F32))
+    made = pl.pallas_call(
         functools.partial(body, sizes),
-        out_shape=(tile_out, tile_out, tile_out, jax.ShapeDtypeStruct((part, CH), F32)),
+        out_shape=outs,
         in_specs=[hbm] * 14,
         out_specs=(vmem,) * 4,
         scratch_shapes=scratch,
         compiler_params=pltpu.CompilerParams(
-            collective_id=0, has_side_effects=True, vmem_limit_bytes=67043328
+            collective_id=0, has_side_effects=True, vmem_limit_bytes=LIMIT
         ),
         name="neighbourhood",
     )(*flat, out_weight, occupancy.reshape(1, 2), *(jnp.asarray(t) for t in fixed))
+    grad_q, grad_k, grad_v, grad_w = pl.pallas_call(
+        deliver,
+        out_shape=outs,
+        in_specs=[hbm] * 4,
+        out_specs=(hbm,) * 4,
+        scratch_shapes=[pltpu.VMEM(o.shape, o.dtype) for o in outs]
+        + [pltpu.SemaphoreType.DMA((4,)), pltpu.SemaphoreType.DMA((4,))],
+        compiler_params=pltpu.CompilerParams(vmem_limit_bytes=LIMIT),
+        name="deliver",
+    )(*made)
     shape = (1, HIGH, WIDE, CH)
     return grad_q.reshape(shape), grad_k.reshape(shape), grad_v.reshape(shape), grad_w
 

time: 78.5 us -> 69.6 us (0.89)
  local copies, waits for them, and re-layouts: 4.83 us -> 0 us
  Pallas kernels: 72.8 us -> 68.8 us
    unnamed x8 -> x0, local copies, waits for them, and re-layouts: 4.83 us -> none
    pallas_call x1 -> x2, Pallas kernels: 72.8 us -> 68.8 us  [the longest x1 66.6 us: on_device(): pl.pallas_call(functools.partial(body, sizes), out_shape=outs, in_specs=[...]
where the time goes in v3:
time: 69.6 us; the launch traced here: 69.5 us
  Pallas kernels  68.8 us (99%)
    pallas_call x1, Pallas kernels, on_device(): pl.pallas_call(functools.partial(body, sizes), out_shape=outs, in_specs=[...  66.6 us
    pallas_call x1, Pallas kernels, on_device(): pl.pallas_call(deliver, out_shape=outs, in_specs=[hbm] * 4, out_specs=(hb...  2.24 us

profile of v3, /device:TPU:5, one launch (start us, length us, event | category | flops | bytes accessed | tf_op | source)
XLA Modules:
  0.0 69.5 jit_solution(6176429147993536881)
XLA Ops:
  0.6 66.6 %neighbourhood.1 = (bf16[128,768]{1,0:T(8,128)(2,1)}, bf16[128,768]{1,0:T(8,128)(2,1)}, bf16[128,768]{1,0:T(8,128)(2,1)}, f32[192,768]{1,0:T(8,128)}) custom-call(bf16[128,768]{1,0:T(8,128)(2,1)} %bitcast.8, bf16[128,768]{1,0:T(8,128)(2,1)} %bitcast.9, bf16[128,768]{1,0:T(8,128)(2,1)} %bitcast.10, bf16[128,768]{1,0:T(8,128)(2,1)} %bitcast.11, ...), custom_call_target="tpu_custom_call" | custom-call | tf_op jit(solution)/shard_map/neighbourhood/pallas_call | solution.py:584
  67.2 2.2 %deliver.1 = (bf16[128,768]{1,0:T(8,128)(2,1)}, bf16[128,768]{1,0:T(8,128)(2,1)}, bf16[128,768]{1,0:T(8,128)(2,1)}, f32[192,768]{1,0:T(8,128)}) custom-call(bf16[128,768]{1,0:T(8,128)(2,1)} %get-tuple-element.12.refs_0_, bf16[128,768]{1,0:T(8,128)(2,1)} %get-tuple-element.13.refs_1_, bf16[128,768]{1,0:T(8,128)(2,1)} %get-tuple-element.14.refs_2_, ...), custom_call_target="tpu_custom_call" | custom-call | tf_op jit(solution)/shard_map/deliver/pallas_call | solution.py:595

commit v4 on v3

--- a/solution.py
+++ b/solution.py
@@ -37,12 +37,13 @@
 def tables():
     places = key_places()
     limit = np.full((KEYS, TILES), 1000.0, np.float32)
-    block = np.zeros((KEYS, 96), np.float32)
+    block = np.zeros((KEYS, 48), np.float32)
     for u, place in enumerate(places):
         if place is None:
             continue
         row, column = place
-        block[u, 8 * (4 * (row // SIDE + 1) + column // SIDE + 1)] = 1
+        across = column // SIDE if u < SIDES else int(column > 0)
+        block[u, 8 * (2 * (row // SIDE + 1) + across)] = 1
         for t in range(TILES):
             if abs(t // WIDE - row) <= REACH and abs(t % WIDE - column) <= REACH:
                 limit[u, t] = (row % SIDE) * SIDE + column % SIDE
@@ -97,7 +98,7 @@
     dq_ref, dk_ref, dv_ref, gw_ref,
     q_ref, go_ref, w_ref, occ_ref,
     limit_ref, block_ref, pack_ref, corners_ref, sides_ref, bcorn_ref, bstrip_ref, unpack_ref,
-    kall, vall, strips, held, corn, cnt, wfull, bias, prob, attn_t, gated,
+    kall, vall, strips, held, corn, cnt, beside, wfull, bias, prob, peak, mass, attn_t, gated,
     dk_own, dv_own, row_out, row_in, dcol, bcorn, bcorn_in, bstrip, bstrip_in,
     gw_own, core_out, core_in, xy_sum, y_out, y_in, x_out, x_in, half_sum, half_out, e_in, z_out, z_in, h_all, g_all,
     ssem, rsem, lsem, far,
@@ -158,6 +159,7 @@
     bcorn_in[...] = jnp.zeros(bcorn_in.shape, BF)
     bstrip_in[...] = jnp.zeros(bstrip_in.shape, BF)
     cnt[...] = jnp.zeros(cnt.shape, F32)
+    beside[...] = jnp.zeros(beside.shape, F32)
 
     barrier = pltpu.get_barrier_semaphore()
 
@@ -174,8 +176,8 @@
     for load in loads[:4]:
         load.wait()
     count0, count1 = occ_ref[0, 0].astype(F32), occ_ref[0, 1].astype(F32)
-    cnt[1, 1] = jnp.full((8, 128), count0, F32)
-    cnt[1, 2] = jnp.full((8, 128), count1, F32)
+    cnt[1, 0] = jnp.full((8, 128), count0, F32)
+    cnt[1, 1] = jnp.full((8, 128), count1, F32)
     packed = dot(pack_ref[:, :TILES], kall[own, :]) + dot(pack_ref[:, TILES:], vall[own, :])
     strips[...] = packed.astype(BF)
 
@@ -225,12 +227,14 @@
     to_up = dict(sends=has_up, gets=has_down)
     to_down = dict(sends=has_down, gets=has_up)
     first = [
-        send(cnt.at[1, 1], cnt.at[1, 3], left, **to_left),
-        send(cnt.at[1, 2], cnt.at[1, 0], right, **to_right),
+        send(cnt.at[1, 0], beside.at[1, 1], left, **to_left),
+        send(cnt.at[1, 1], beside.at[1, 0], right, **to_right),
         send(strips.at[pl.ds(0, 48)], held.at[pl.ds(48, 48)], left, **to_left),
         send(strips.at[pl.ds(48, 48)], held.at[pl.ds(0, 48)], right, **to_right),
     ]
     rows = [
+        send(cnt.at[1], cnt.at[2], up, **to_up),
+        send(cnt.at[1], cnt.at[0], down, **to_down),
         send(kall.at[pl.ds(0, 48)], kall.at[pl.ds(DOWN, 48)], up, **to_up),
         send(kall.at[pl.ds(80, 48)], kall.at[pl.ds(UP, 48)], down, **to_down),
         send(vall.at[pl.ds(0, 48)], vall.at[pl.ds(DOWN, 48)], up, **to_up),
@@ -241,14 +245,58 @@
     base = pl.multiple_of(dp * part, 16)
     wfull[pl.ds(base, part), :] = w_ref[...]
 
+    lane = lax.broadcasted_iota(jnp.int32, (1, 128), 1)
+    low = (lane < 64).astype(F32).astype(BF)
+    high = (lane >= 64).astype(F32).astype(BF)
+
+    def occupied(index):
+        place = ((index >> 4) * 8 + (index & 7)).astype(F32)
+        count = jnp.where(((index >> 3) & 1) == 0, count0, count1)
+        return (place < count).astype(F32)
+
+    valid_lane = occupied(lane)
+    valid_row = occupied(lax.broadcasted_iota(jnp.int32, (TILES, CH), 0))
+
+    def both(value):
+        return jnp.concatenate([value * low, value * high], axis=0)
+
+    def own_heads(value):
+        return jnp.concatenate([value[:64, :TILES], value[64:, TILES:]], axis=0)
+
+    def lanes(p):
+        if isinstance(p, int):
+            return pl.ds(p * PAIR, PAIR)
+        return pl.ds(pl.multiple_of(p * PAIR, PAIR), PAIR)
+
+    for copy in rows:
+        copy.arrived()
+
+    def set_bias(first, count, table):
+        counts = dot(block_ref[pl.ds(first, count), :], table[...].reshape(48, 128).astype(BF))
+        near = jnp.where(limit_ref[pl.ds(first, count), :].astype(F32) < counts, 0.0, NEG)
+        bias[pl.ds(first, count), :TILES] = near
+        bias[pl.ds(first, count), TILES:] = near
+
+    set_bias(0, SIDES, cnt)
+
+    @pl.loop(0, PAIRS)
+    def _(p):
+        queries = both(q_ref[:, lanes(p)])
+        scores = dot(kall[pl.ds(0, SIDES), lanes(p)], queries, ((1,), (1,))) * HEAD_SCALE + bias[:SIDES, :]
+        highest = jnp.max(scores, axis=0, keepdims=True)
+        raised = jnp.exp(scores - highest)
+        prob[p, :SIDES, :] = raised
+        peak[p] = jnp.broadcast_to(highest, (8, 2 * TILES))
+        mass[p] = jnp.broadcast_to(jnp.sum(raised, axis=0, keepdims=True), (8, 2 * TILES))
+
     for copy in first:
         copy.arrived()
     corn[...] = dot(corners_ref[...], held[pl.ds(0, 96), :]).astype(BF)
     second = [
         send(corn.at[pl.ds(0, 48)], held.at[pl.ds(144, 48)], up, **to_up),
         send(corn.at[pl.ds(48, 48)], held.at[pl.ds(96, 48)], down, **to_down),
-        send(cnt.at[1], cnt.at[2], up, **to_up),
-        send(cnt.at[1], cnt.at[0], down, **to_down),
+        send(beside.at[1], beside.at[2], up, **to_up),
+        send(beside.at[1], beside.at[0], down, **to_down),
     ]
 
     gathers = []
@@ -259,44 +307,22 @@
             send(w_ref.at[pl.ds(own_at, size)], wfull.at[pl.ds(at, size)], along_z(step))
         )
 
-    for copy in rows + second:
+    for copy in second:
         copy.arrived()
     side_keys = dot(sides_ref[...], held[...])
     kall[pl.ds(SIDES, 96), :] = side_keys[:96].astype(BF)
     vall[pl.ds(SIDES, 96), :] = side_keys[96:].astype(BF)
-    counts = dot(block_ref[...], cnt[...].reshape(96, 128).astype(BF))
-    near = jnp.where(limit_ref[...].astype(F32) < counts, 0.0, NEG)
-    bias[:, :TILES] = near
-    bias[:, TILES:] = near
-
-    lane = lax.broadcasted_iota(jnp.int32, (1, 128), 1)
-    low = (lane < 64).astype(F32).astype(BF)
-    high = (lane >= 64).astype(F32).astype(BF)
-
-    def occupied(index):
-        place = ((index >> 4) * 8 + (index & 7)).astype(F32)
-        count = jnp.where(((index >> 3) & 1) == 0, count0, count1)
-        return (place < count).astype(F32)
-
-    valid_lane = occupied(lane)
-    valid_row = occupied(lax.broadcasted_iota(jnp.int32, (TILES, CH), 0))
-
-    def both(value):
-        return jnp.concatenate([value * low, value * high], axis=0)
-
-    def own_heads(value):
-        return jnp.concatenate([value[:64, :TILES], value[64:, TILES:]], axis=0)
-
-    def lanes(p):
-        if isinstance(p, int):
-            return pl.ds(p * PAIR, PAIR)
-        return pl.ds(pl.multiple_of(p * PAIR, PAIR), PAIR)
+    set_bias(SIDES, KEYS - SIDES, beside)
 
     def forward(p):
-        keys, values = kall[:, lanes(p)], vall[:, lanes(p)]
-        scores = dot(keys, both(q_ref[:, lanes(p)]), ((1,), (1,))) * HEAD_SCALE + bias[...]
-        raised = jnp.exp(scores - jnp.max(scores, axis=0, keepdims=True))
-        weights = raised * (1.0 / jnp.sum(raised, axis=0, keepdims=True))
+        keys, values = kall[pl.ds(SIDES, KEYS - SIDES), lanes(p)], vall[:, lanes(p)]
+        scores = dot(keys, both(q_ref[:, lanes(p)]), ((1,), (1,))) * HEAD_SCALE + bias[SIDES:, :]
+        before = peak[p][:1]
+        highest = jnp.maximum(before, jnp.max(scores, axis=0, keepdims=True))
+        raised = jnp.exp(scores - highest)
+        scale = jnp.exp(before - highest)
+        inverse = 1.0 / (scale * mass[p][:1] + jnp.sum(raised, axis=0, keepdims=True))
+        weights = jnp.concatenate([prob[p, :SIDES, :] * (scale * inverse), raised * inverse], axis=0)
         prob[p] = weights
         mixed = own_heads(dot(values, weights.astype(BF), ((0,), (0,))))
         attn_t[pl.ds(pl.multiple_of(p * PAIR, PAIR), PAIR), :] = (mixed * valid_lane).astype(BF)
@@ -418,11 +444,11 @@
         total = total + e_in[s - 1].astype(F32)
     z_out[...] = total.astype(BF)
     keeper = dp == x
-    z_copies = []
-    for s in range(1, DP):
-        z_copies.append(
-            send(z_out, z_in.at[s - 1], ((dp + s) % DP, row, col), sends=(dp + s) % DP == x, gets=keeper)
-        )
+    behind = (z + Z - x) % DP
+    z_copies = [
+        send(z_out, z_in.at[i], along_z(step), sends=behind == (DP - step) % DP, gets=keeper)
+        for i, step in enumerate((-1, 1, -2))
+    ]
 
     run(5, 6)
     bcorn[...] = dot(bcorn_ref[...], dcol[...]).astype(BF)
@@ -544,10 +570,13 @@
         pltpu.VMEM((96, CH), BF),
         pltpu.VMEM((192, CH), BF),
         pltpu.VMEM((96, CH), BF),
-        pltpu.VMEM((3, 4, 8, 128), F32),
+        pltpu.VMEM((3, 2, 8, 128), F32),
+        pltpu.VMEM((3, 2, 8, 128), F32),
         pltpu.VMEM((CH, CH), BF),
         pltpu.VMEM((KEYS, 2 * TILES), F32),
         pltpu.VMEM((PAIRS, KEYS, 2 * TILES), F32),
+        pltpu.VMEM((PAIRS, 8, 2 * TILES), F32),
+        pltpu.VMEM((PAIRS, 8, 2 * TILES), F32),
         pltpu.VMEM((CH, TILES), BF),
         pltpu.VMEM((TILES, CH), BF),
         pltpu.VMEM((TILES, CH), F32),

time: 69.6 us -> 68.7 us (0.987)
  Pallas kernels: 68.8 us -> 67.9 us
    pallas_call x1, Pallas kernels: 66.6 us -> 65.6 us  [on_device(): pl.pallas_call(functools.partial(body, sizes), out_shape=outs, in_specs=[...]
where the time goes in v4:
time: 68.7 us; the launch traced here: 68.5 us
  Pallas kernels  67.9 us (99%)
    pallas_call x1, Pallas kernels, on_device(): pl.pallas_call(functools.partial(body, sizes), out_shape=outs, in_specs=[...  65.6 us
    pallas_call x1, Pallas kernels, on_device(): pl.pallas_call(deliver, out_shape=outs, in_specs=[hbm] * 4, out_specs=(hb...  2.24 us

profile of v4, /device:TPU:5, one launch (start us, length us, event | category | flops | bytes accessed | tf_op | source)
XLA Modules:
  0.0 68.5 jit_solution(18124599322204077160)
XLA Ops:
  0.6 65.6 %neighbourhood.1 = (bf16[128,768]{1,0:T(8,128)(2,1)}, bf16[128,768]{1,0:T(8,128)(2,1)}, bf16[128,768]{1,0:T(8,128)(2,1)}, f32[192,768]{1,0:T(8,128)}) custom-call(bf16[128,768]{1,0:T(8,128)(2,1)} %bitcast.8, bf16[128,768]{1,0:T(8,128)(2,1)} %bitcast.9, bf16[128,768]{1,0:T(8,128)(2,1)} %bitcast.10, bf16[128,768]{1,0:T(8,128)(2,1)} %bitcast.11, ...), custom_call_target="tpu_custom_call" | custom-call | tf_op jit(solution)/shard_map/neighbourhood/pallas_call | solution.py:613
  66.2 2.2 %deliver.1 = (bf16[128,768]{1,0:T(8,128)(2,1)}, bf16[128,768]{1,0:T(8,128)(2,1)}, bf16[128,768]{1,0:T(8,128)(2,1)}, f32[192,768]{1,0:T(8,128)}) custom-call(bf16[128,768]{1,0:T(8,128)(2,1)} %get-tuple-element.12.refs_0_, bf16[128,768]{1,0:T(8,128)(2,1)} %get-tuple-element.13.refs_1_, bf16[128,768]{1,0:T(8,128)(2,1)} %get-tuple-element.14.refs_2_, ...), custom_call_target="tpu_custom_call" | custom-call | tf_op jit(solution)/shard_map/deliver/pallas_call | solution.py:624

commit v5 on v4

--- a/solution.py
+++ b/solution.py
@@ -509,6 +509,7 @@
     for copy in spread:
         copy.arrived()
     spread_y = [send(own_piece, own_piece, along_y(s)) for s in range(1, Y)]
+    core_back = [send(own_piece, own_piece, partner)]
 
     for copy in back_strips:
         copy.arrived()
@@ -517,10 +518,12 @@
         side_term = dot(unpack_ref[pl.ds(TILES * kind, TILES), :], edge)
         out[...] = (total[...] + side_term).astype(BF)
 
-    for copy in spread_y:
-        copy.arrived()
-    core_back = send(g_all.at[core], g_all.at[core], partner)
-    core_back.arrived()
+    for s, copy in zip(range(1, Y), spread_y):
+        copy.arrived()
+        piece = g_all.at[core, (y + Y - s) % Y]
+        core_back.append(send(piece, piece, partner))
+    for copy in core_back:
+        copy.arrived()
     norm = (TILES * DP * ROWS * COLS) ** (-0.5)
     for c in range(2):
         for j in range(Y):
@@ -531,7 +534,7 @@
         copy.sent()
 
 
-COPIES = 64
+COPIES = 72
 UNROLLED = False
 LIMIT = 67043328
 

time: 68.7 us -> 68.7 us (level)
  no operation moved by 1% of the time
where the time goes in v5:
time: 68.7 us; the launch traced here: 68.5 us
  Pallas kernels  67.9 us (99%)
    pallas_call x1, Pallas kernels, on_device(): pl.pallas_call(functools.partial(body, sizes), out_shape=outs, in_specs=[...  65.6 us
    pallas_call x1, Pallas kernels, on_device(): pl.pallas_call(deliver, out_shape=outs, in_specs=[hbm] * 4, out_specs=(hb...  2.24 us

profile of v5, /device:TPU:5, one launch (start us, length us, event | category | flops | bytes accessed | tf_op | source)
XLA Modules:
  0.0 68.5 jit_solution(991988883703553744)
XLA Ops:
  0.6 65.6 %neighbourhood.1 = (bf16[128,768]{1,0:T(8,128)(2,1)}, bf16[128,768]{1,0:T(8,128)(2,1)}, bf16[128,768]{1,0:T(8,128)(2,1)}, f32[192,768]{1,0:T(8,128)}) custom-call(bf16[128,768]{1,0:T(8,128)(2,1)} %bitcast.8, bf16[128,768]{1,0:T(8,128)(2,1)} %bitcast.9, bf16[128,768]{1,0:T(8,128)(2,1)} %bitcast.10, bf16[128,768]{1,0:T(8,128)(2,1)} %bitcast.11, ...), custom_call_target="tpu_custom_call" | custom-call | tf_op jit(solution)/shard_map/neighbourhood/pallas_call | solution.py:616
  66.3 2.2 %deliver.1 = (bf16[128,768]{1,0:T(8,128)(2,1)}, bf16[128,768]{1,0:T(8,128)(2,1)}, bf16[128,768]{1,0:T(8,128)(2,1)}, f32[192,768]{1,0:T(8,128)}) custom-call(bf16[128,768]{1,0:T(8,128)(2,1)} %get-tuple-element.12.refs_0_, bf16[128,768]{1,0:T(8,128)(2,1)} %get-tuple-element.13.refs_1_, bf16[128,768]{1,0:T(8,128)(2,1)} %get-tuple-element.14.refs_2_, ...), custom_call_target="tpu_custom_call" | custom-call | tf_op jit(solution)/shard_map/deliver/pallas_call | solution.py:627
